TPU v7x, 512 devices: a whole 4x4x16 slice. The times are simulated.
512 devices in a mesh: dp: 32 (over y, x, core), table: 16 (over z).
Axes of the slice: x: 4, y: 4, z: 16, core: 2. Of those that a mesh axis runs over, the one named last changes fastest.
Arguments:
- hidden_in: bfloat16 [4096, 4096], P('dp', 'table'), may hold values from -6 to 6
- gate_weight: bfloat16 [4096, 4096], P('dp', 'table'), may hold values from -0.09375 to 0.09375
- values: bfloat16 [2048, 4096], P('table'), may hold values from -6 to 6
- pick_rows: int32 [4096, 32], P('dp'), may hold values from 0 to 2047, all different within a row
- pick_scores: float32 [4096, 32], P('dp'), may hold values from -300 to 300
- grad_out: bfloat16 [4096, 4096], P('dp', 'table'), may hold values from -6 to 6
Outputs:
- branch_out: bfloat16 [4096, 4096], P('dp', 'table')
- grad_hidden: bfloat16 [4096, 4096], P('dp', 'table')
- grad_gate: float32 [4096, 4096], P('dp', 'table')
- grad_values: float32 [2048, 4096], P('table')
- grad_scores: float32 [4096, 32], P('dp')
Inputs may be any that keep to these rules, and one draw needn't show every extreme that they name: `pick_rows`: the 32 rows of a token are distinct.
All inputs are finite; a program needn't handle non-finite values.
Results may differ from a plain program's by a relative error of at most 0.025.
Values may be sent and summed in bfloat16 or wider, within the bound.
A program may use at most 64 MiB of HBM per device.

v0:
```python
import jax
import jax.numpy as jnp
from jax import lax
from jax.sharding import PartitionSpec as P


def pick_weights(pick_scores):
    row_max = jnp.max(pick_scores, axis=1, keepdims=True)
    exponent = jnp.exp(pick_scores - row_max)
    return exponent / jnp.sum(exponent, axis=1, keepdims=True)


def spread_weights(row_ids, weights_bf, row_total):
    token_ids = lax.broadcasted_iota(jnp.int32, row_ids.shape, 0)
    empty = jnp.zeros((row_ids.shape[0], row_total), jnp.bfloat16)
    return empty.at[token_ids, row_ids].set(weights_bf, mode="drop")


def local(hidden_in, gate_weight, values, pick_rows, pick_scores, grad_out):
    weights = pick_weights(pick_scores)
    weights_bf = weights.astype(jnp.bfloat16)
    token_count = hidden_in.shape[0]
    col_count = hidden_in.shape[1]
    rows_here = values.shape[0]
    whole_in = lax.all_gather(hidden_in, "table", axis=1, tiled=True)
    weight_full = lax.all_gather(gate_weight, "dp", axis=0, tiled=True)
    local_rows = pick_rows - lax.axis_index("table") * rows_here
    owned = (local_rows >= 0) & (local_rows < rows_here)
    parked = jnp.where(owned, local_rows, rows_here)
    spread = spread_weights(parked, weights_bf, rows_here)
    partial_mem = jnp.dot(spread, values, preferred_element_type=jnp.float32)
    arrived = lax.all_to_all(
        partial_mem.astype(jnp.bfloat16), "table", split_axis=1, concat_axis=0, tiled=True
    ).astype(partial_mem.dtype)
    memory_read = jnp.sum(arrived.reshape(-1, token_count, col_count), axis=0)
    gate_input = jnp.dot(whole_in, weight_full, preferred_element_type=jnp.float32)
    sigmoid_v = jax.nn.sigmoid(gate_input)
    gate_value = gate_input * sigmoid_v
    gate_slope = sigmoid_v * (1.0 + gate_input * (1.0 - sigmoid_v))
    branch_out = (memory_read * gate_value).astype(jnp.bfloat16)
    upstream = grad_out.astype(jnp.float32)
    mem_grad = (upstream * gate_value).astype(jnp.bfloat16)
    gate_grad_in = (upstream * memory_read * gate_slope).astype(jnp.bfloat16)
    grad_full = lax.all_gather(mem_grad, "table", axis=1, tiled=True)
    value_term = lax.dot_general(
        spread, grad_full, (((0,), (0,)), ((), ())), preferred_element_type=jnp.float32
    )
    affinity_all = lax.dot_general(
        grad_full, values, (((1,), (1,)), ((), ())), preferred_element_type=jnp.float32
    )
    picked = jnp.take_along_axis(affinity_all, jnp.where(owned, local_rows, 0), axis=1)
    affinity_part = jnp.where(owned, picked, 0.0)
    affinity = lax.psum(affinity_part, "table")
    grad_scores = weights * (affinity - jnp.sum(weights * affinity, axis=1, keepdims=True))
    grad_values = lax.psum(value_term.astype(jnp.bfloat16), "dp").astype(jnp.float32)
    grad_gate = lax.psum_scatter(
        lax.dot_general(
            whole_in, gate_grad_in, (((0,), (0,)), ((), ())), preferred_element_type=jnp.float32
        ).astype(jnp.bfloat16),
        "dp",
        scatter_dimension=0,
        tiled=True,
    ).astype(jnp.float32)
    input_term = lax.dot_general(
        gate_grad_in, weight_full, (((1,), (1,)), ((), ())), preferred_element_type=jnp.float32
    )
    grad_hidden = lax.psum_scatter(
        input_term.astype(jnp.bfloat16), "table", scatter_dimension=1, tiled=True
    )
    return (branch_out, grad_hidden, grad_gate, grad_values, grad_scores)


def solution(mesh):
    placed = (
        P("dp", "table"),
        P("dp", "table"),
        P("table", None),
        P("dp", None),
        P("dp", None),
        P("dp", "table"),
    )
    return jax.shard_map(
        local,
        mesh=mesh,
        in_specs=placed,
        out_specs=(
            P("dp", "table"),
            P("dp", "table"),
            P("dp", "table"),
            P("table", None),
            P("dp", None),
        ),
        check_vma=False,
    )
```

profile of v0, /device:TPU:1, one launch (start us, length us, event | category | flops | bytes accessed | tf_op | source)
XLA Modules:
  0.0 561.6 jit_solution(2590282525393934483)
XLA Ops:
  7.2 0.0 all-gather.4.cloned.1.call-start
  7.2 0.7 all-gather.4.cloned.1.call-update
  7.9 0.8 copy.22
  8.8 0.1 copy.23
  8.9 0.7 multiply_reduce_fusion.1
  9.6 0.1 copy.24
  9.7 0.1 reshape.49
  9.8 0.8 copy.25
  10.6 0.7 reduce_max.9
  11.3 0.2 fusion.7
  11.5 0.1 fusion.12
  11.7 0.1 reshape.51
  11.7 28.6 %scatter_custom_fusion = bf16[16384]{0:T(1024)(128)(2,1)S(1)} fusion(s32[4096]{0:T(1024)S(1)} %reshape.49, bf16[4096]{0:T(1024)(128)(2,1)S(1)} %reshape.51, bf16[]{:T(256)} %constant.9.clone.1), kind=kCustom, calls=%fused_computation.33 | custom fusion | bytes 32770
  40.4 0.4 convolution_convert_fusion.3
  40.8 1.1 copy.33
  41.9 15.9 %all-to-all-start = ((bf16[128,16,256]{2,0,1:T(8,128)(2,1)}), bf16[128,16,256]{2,0,1:T(8,128)(2,1)S(1)}, u32[]{:S(2)}, u32[]{:S(2)}) async-start(bf16[128,16,256]{2,0,1:T(8,128)(2,1)} %bitcast.27), calls=%async_computation | async-start | bytes 2097152 | tf_op jit(solution)/shard_map/all_to_all | solution.py:32
  57.8 0.0 all-gather.6.cloned.1.call-start
  57.8 0.7 all-gather.6.cloned.1.call-update
  58.5 0.0 all-gather.8.cloned.1.call-start
  58.6 48.3 %all-to-all-done = bf16[128,16,256]{2,0,1:T(8,128)(2,1)S(1)} async-done(((bf16[128,16,256]{2,0,1:T(8,128)(2,1)}), bf16[128,16,256]{2,0,1:T(8,128)(2,1)S(1)}, u32[]{:S(2)}, u32[]{:S(2)}) %all-to-all-start) | async-done | bytes 1048608 | tf_op jit(solution)/shard_map/all_to_all | solution.py:32
  106.8 0.1 convert_reduce_fusion
  107.0 0.8 all-gather.4.cloned.1.call-done
  107.8 67.3 %all-gather.6.cloned.1.call-done = bf16[4096,256]{1,0:T(8,128)(2,1)} async-done(((bf16[128,256]{1,0:T(8,128)(2,1)}), bf16[4096,256]{1,0:T(8,128)(2,1)}) %all-gather.6.cloned.1.call-update) | async-done | bytes 2097168 | tf_op jit(solution)/shard_map/all_gather | solution.py:26
  175.0 3.1 fusion.2
  178.1 0.0 all-gather.8.cloned.1.call-update
  178.1 0.0 all-reduce.2.cloned.1.call-start
  178.2 60.1 %all-gather.8.cloned.1.call-done = bf16[128,4096]{1,0:T(8,128)(2,1)} async-done(((bf16[128,256]{1,0:T(8,128)(2,1)}), bf16[128,4096]{1,0:T(8,128)(2,1)}) %all-gather.8.cloned.1.call-update) | async-done | bytes 1048592 | tf_op jit(solution)/shard_map/all_gather | solution.py:44
  238.3 2.7 convolution_convert_fusion.1
  240.9 0.0 all-reduce.2.cloned.1.call-update
  241.0 0.0 reduce-scatter.7.cloned.1.call-start
  241.0 2.0 fusion
  243.0 2.5 copy.29
  245.5 0.0 reduce-scatter.5.cloned.1.call-start
  245.5 3.5 convolution_convert_fusion.2
  249.1 0.1 reshape.43
  249.2 0.4 fusion.13
  249.6 25.6 %gather_fusion = f32[4096]{0:T(1024)S(1)} fusion(f32[128,128]{1,0:T(8,128)S(1)} %fusion.13, s32[4096]{0:T(1024)S(1)} %reshape.43), kind=kCustom, calls=%fused_computation | custom fusion | bytes 65536 | tf_op jit(solution)/shard_map/jit(take_along_axis)/gather | solution.py:51
  275.2 0.1 reshape.46
  275.4 41.2 %psum.15 = f32[128,32]{1,0:T(8,128)S(1)} all-reduce(f32[128,32]{1,0:T(8,128)S(1)} %select_select_fusion), channel_id=1, replica_groups=mesh['dp'=32,'table'=16] {'table'}, use_global_device_ids=true, to_apply=%region_7.8 | all-reduce | flops 4096 | bytes 32768 | tf_op jit(solution)/shard_map/psum | solution.py:53
  316.6 0.2 multiply_reduce_fusion
  316.8 0.1 subtract_multiply_fusion
  316.9 0.7 copy.28
  317.6 66.9 %all-reduce.2.cloned.1.call-done = bf16[128,4096]{1,0:T(8,128)(2,1)} async-done(((bf16[128,4096]{1,0:T(8,128)(2,1)}), bf16[128,4096]{1,0:T(8,128)(2,1)}) %all-reduce.2.cloned.1.call-update) | async-done | bytes 1048592 | tf_op jit(solution)/shard_map/psum | solution.py:55
  384.5 2.8 convert_element_type.53
  387.3 102.4 %reduce-scatter.7.cloned.1.call-done = bf16[128,256]{1,0:T(8,128)(2,1)} async-done(((bf16[4096,256]{1,0:T(8,128)(2,1)}), bf16[128,256]{1,0:T(8,128)(2,1)}) %reduce-scatter.7.cloned.1.call-update) | async-done | bytes 65552
  489.7 0.9 copy.30
  490.6 0.8 copy.27
  491.4 63.4 %reduce-scatter.5.cloned.1.call-done = bf16[128,256]{1,0:T(8,128)(2,1)} async-done(((bf16[128,4096]{1,0:T(8,128)(2,1)}), bf16[128,256]{1,0:T(8,128)(2,1)}) %reduce-scatter.5.cloned.1.call-update) | async-done | bytes 65552 | tf_op jit(solution)/shard_map/reduce_scatter | solution.py:67
  (14 shorter events, 0.2 us)
Async XLA Ops:
  7.2 33.2 %copy-start = (bf16[128,4096]{1,0:T(8,128)(2,1)S(1)}, bf16[128,4096]{1,0:T(8,128)(2,1)}, u32[]{:S(2)}) copy-start(bf16[128,4096]{1,0:T(8,128)(2,1)} %param.8) | copy-start | bytes 3145732
  7.2 100.6 %all-gather.4.cloned.1.call-start = ((), (), s32[]{:S(2)}) async-start(), calls=%async_computation.3 | async-start | bytes 1114112 | tf_op jit(solution)/shard_map/all_gather | solution.py:25
  41.9 133.2 %copy-start.2 = (bf16[128,256]{1,0:T(8,128)(2,1)S(1)}, bf16[128,256]{1,0:T(8,128)(2,1)}, u32[]{:S(2)}) copy-start(bf16[128,256]{1,0:T(8,128)(2,1)} %param.11) | copy-start | bytes 196612
  41.9 65.0 %all-to-all-start = ((bf16[128,16,256]{2,0,1:T(8,128)(2,1)}), bf16[128,16,256]{2,0,1:T(8,128)(2,1)S(1)}, u32[]{:S(2)}, u32[]{:S(2)}) async-start(bf16[128,16,256]{2,0,1:T(8,128)(2,1)} %bitcast.27), calls=%async_computation | async-start | bytes 2097152 | tf_op jit(solution)/shard_map/all_to_all | solution.py:32
  57.8 117.3 %all-gather.6.cloned.1.call-start = ((), (), s32[]{:S(2)}) async-start(), calls=%async_computation.4 | async-start | bytes 2162688 | tf_op jit(solution)/shard_map/all_gather | solution.py:26
  58.5 179.8 %all-gather.8.cloned.1.call-start = ((), (), s32[]{:S(2)}) async-start(), calls=%async_computation.6 | async-start | bytes 1114112 | tf_op jit(solution)/shard_map/all_gather | solution.py:44
  178.1 206.4 %all-reduce.2.cloned.1.call-start = ((), (), s32[]{:S(2)}) async-start(), calls=%async_computation.7 | async-start | bytes 2097152 | tf_op jit(solution)/shard_map/psum | solution.py:55
  241.0 248.7 %reduce-scatter.7.cloned.1.call-start = ((), (), s32[]{:S(2)}) async-start(), calls=%async_computation.8 | async-start | bytes 2162688
  245.5 3.7 copy-start.1
  245.5 309.3 %reduce-scatter.5.cloned.1.call-start = ((), (), s32[]{:S(2)}) async-start(), calls=%async_computation.5 | async-start | bytes 1114112 | tf_op jit(solution)/shard_map/reduce_scatter | solution.py:67
Sparse Core Ops, SparseCore 0:
  10.0 97.7 all-gather.3
  110.9 64.0 all-gather.5
  178.3 59.9 all-gather.7
  241.9 142.5 all-reduce.1
  389.4 100.1 reduce-scatter.6
  493.1 61.5 reduce-scatter.4
where the time goes:
time: 571 us; the launch traced here: 562 us
  waiting for transfers between devices  411 us (72%)
  local copies, waits for them, and re-layouts  62.3 us (11%)
  blocking collectives  41.2 us (7%)
  starting transfers between devices  16.1 us (3%)
  between operations  14.3 us (3%)
  matrix products  12 us (2%)
    unnamed x7, waiting for transfers between devices  104 us
    all_gather x1, waiting for transfers between devices, local(): weight_full = lax.all_gather(gate_weight, 'dp', axis=0, tiled=True)  67.3 us
    psum x1, waiting for transfers between devices, local(): lax.psum(value_term.astype(jnp.bfloat16), 'dp').astype(jnp.float32)  66.9 us
    reduce_scatter x1, waiting for transfers between devices, local(): lax.psum_scatter(input_term.astype(jnp.bfloat16), 'table', scatter_dimens...  63.4 us
    all_gather x1, waiting for transfers between devices, local(): grad_full = lax.all_gather(mem_grad, 'table', axis=1, tiled=True)  60.1 us
    all_to_all x1, waiting for transfers between devices, local(): lax.all_to_all(partial_mem.astype(jnp.bfloat16), 'table', split_axis=1, c...  48.3 us
    psum x1, blocking collectives, local(): affinity = lax.psum(affinity_part, 'table')  41.2 us
    unnamed x15, local copies, waits for them, and re-layouts  35.3 us
  transfers between devices with their start and end apart: 7, of which 7 were waited for; matrix products, arithmetic and copies ran while one was open for 13% of the time, Pallas kernels for 0%

commit v1 on v0

v1 whole, which is shorter than its diff:
```python
import functools
import heapq

import jax
import jax.numpy as jnp
from jax import lax
from jax.experimental import pallas as pl
from jax.experimental.pallas import tpu as pltpu
from jax.sharding import PartitionSpec as P

MESH_ID = pl.DeviceIdType.MESH
F32 = jnp.float32
BF = jnp.bfloat16
NX = 4
NY = 4
CHUNKS = 2
N_COPIES = 256
N_LOCAL = 16
NT = (((1,), (1,)), ((), ()))


def wrap(value, size):
    return lax.rem(value + size, size)


def mult(value, unit):
    return pl.multiple_of(value, unit)


def run_streams(streams):
    heap = []
    for order, stream in enumerate(streams):
        heapq.heappush(heap, (0.0, order, stream))
    while heap:
        when, order, stream = heapq.heappop(heap)
        try:
            due = next(stream)
        except StopIteration:
            continue
        heapq.heappush(heap, (due, order, stream))


def body(
    nz,
    hid_in, w_in, val_in, rows_in, score_in, go_in,
    bo_out, gh_out, gg_out, gv_out, gs_out,
    hid, wts, vals, spread, spread_t, go, gin, mg, gg, pad_a, pad_b, rel_t, wgt, idx,
    pterm, pr0, psum, pr_bundle, pr_piece,
    tterm, tr0, tsum, tr_row, tr_col, tr_piece, tfin, gvals,
    iterm, ri, affp, affr, affall, afft,
    send_sem, recv_sem, local_sem,
):
    rows_blk = hid_in.shape[0]
    cols = hid_in.shape[1]
    b = lax.axis_index("dp")
    z = lax.axis_index("table")
    c = lax.rem(b, 2)
    x = lax.rem(lax.div(b, 2), NX)
    y = lax.div(b, 2 * NX)
    s = 1 - 2 * c
    oc = 1 - c

    def dev(yy, xx, cc):
        return ((yy * NX + xx) * 2 + cc, z)

    def zdev(delta):
        return (b, wrap(z + delta, nz))

    def xdev(delta):
        return dev(y, wrap(x + delta, NX), c)

    def ydev(delta):
        return dev(wrap(y + delta, NY), x, c)

    partner = dev(y, x, oc)

    barrier = pltpu.get_barrier_semaphore()
    peers = [zdev(k) for k in range(1, nz)] + [xdev(1), xdev(-1), ydev(1), ydev(-1), partner]
    for peer in peers:
        pl.semaphore_signal(barrier, inc=1, device_id=peer, device_id_type=MESH_ID)

    local_count = [0]
    copy_count = [0]
    sent = []

    def lcopy(src, dst):
        i = local_count[0]
        local_count[0] += 1
        cp = pltpu.make_async_copy(src, dst, local_sem.at[i])
        cp.start()
        return cp

    def send(src, dst, peer, track=True):
        i = copy_count[0]
        copy_count[0] += 1
        cp = pltpu.make_async_remote_copy(
            src_ref=src, dst_ref=dst, send_sem=send_sem.at[i], recv_sem=recv_sem.at[i],
            device_id=peer, device_id_type=MESH_ID,
        )
        cp.start()
        if track:
            sent.append(cp)
        return cp

    own_w = lcopy(w_in, wts.at[y, x, c])
    own_h = lcopy(hid_in, hid.at[z])
    own_g = lcopy(go_in, go)

    ylow = lax.rem(y, 2)
    yhigh = lax.div(y, 2)

    pad_a[...] = jnp.zeros_like(pad_a)
    pad_b[...] = jnp.zeros_like(pad_b)
    pad_a[:, 0:32] = rows_in[...].astype(F32)
    pad_b[:, 0:32] = score_in[...]
    total_rows = nz * rows_blk

    def relative(row_f):
        shifted = row_f.astype(jnp.int32) + (total_rows - rows_blk * z)
        return jnp.where(shifted >= total_rows, shifted - total_rows, shifted)

    idx[...] = relative(pad_a[...])
    rel_t[...] = relative(pad_a[...].T[0:32, :])
    scores = pad_b[...].T[0:32, :]
    expo = jnp.exp(scores - jnp.max(scores, axis=0, keepdims=True))
    wgt[...] = expo / jnp.sum(expo, axis=0, keepdims=True)
    weights_bf = wgt[...].astype(BF).astype(F32)
    afft[...] = weights_bf

    def spread_block(i, carry):
        ids = lax.broadcasted_iota(jnp.int32, (rows_blk, rows_blk), 0) + i * rows_blk
        acc = jnp.zeros((rows_blk, rows_blk), F32)
        for k in range(32):
            acc = jnp.where(rel_t[k : k + 1, :] == ids, afft[k : k + 1, :], acc)
        spread_t[i] = acc.astype(BF)
        spread[:, pl.ds(mult(i * rows_blk, rows_blk), rows_blk)] = acc.T.astype(BF)
        return carry

    lax.fori_loop(0, nz, spread_block, 0)

    own_w.wait()
    own_h.wait()
    own_g.wait()
    pl.semaphore_wait(barrier, len(peers))

    def w_piece(yy, xx, cc, half):
        return wts.at[yy, xx, cc, :, pl.ds(128 * half, 128)]

    def w_row(yy, cc, half):
        return wts.at[yy, :, cc, :, pl.ds(128 * half, 128)]

    def w_col(xx, cc, half):
        return wts.at[:, xx, cc, :, pl.ds(128 * half, 128)]

    def jset(cc, half):
        return pl.ds(8 * (1 - cc) + 4 * half, 4)

    def hi(yy):
        return pl.ds(mult(128 * lax.div(yy, 2), 128), 128)

    def t_slices(buf):
        def piece(yy, xx, cc, half):
            return buf.at[jset(cc, half), lax.rem(yy, 2), xx, :, hi(yy)]

        def row(yy, cc, half):
            return buf.at[jset(cc, half), lax.rem(yy, 2), :, :, hi(yy)]

        def col(xx, cc, half):
            return buf.at[jset(cc, half), :, xx]

        return piece, row, col

    def plane_gather(slices, half, t0, small, large, done):
        piece, row, col = slices
        if half == 0:
            line = lambda p: piece(y, p, c, half)
            bundle = lambda p, cc: row(p, cc, half)
            pos, near, pos2, near2, n1, n2 = x, xdev, y, ydev, NX, NY
        else:
            line = lambda p: piece(p, x, c, half)
            bundle = lambda p, cc: col(p, cc, half)
            pos, near, pos2, near2, n1, n2 = y, ydev, x, xdev, NY, NX
        up = send(line(pos), line(pos), near(1))
        down = send(line(pos), line(pos), near(-1))
        t = t0 + small
        yield t
        up.wait_recv()
        down.wait_recv()
        back = wrap(pos - s, n1)
        far = send(line(back), line(back), near(s))
        t += small
        yield t
        far.wait_recv()
        ups = send(bundle(pos2, c), bundle(pos2, c), near2(1))
        downs = send(bundle(pos2, c), bundle(pos2, c), near2(-1))
        swap = [send(bundle(pos2, c), bundle(pos2, c), partner)]
        t += large
        yield t
        ups.wait_recv()
        downs.wait_recv()
        back2 = wrap(pos2 - s, n2)
        fars = send(bundle(back2, c), bundle(back2, c), near2(s))
        for step in (-1, 1):
            p = wrap(pos2 + step, n2)
            swap.append(send(bundle(p, c), bundle(p, c), partner))
        t += large
        yield t
        fars.wait_recv()
        p = wrap(pos2 + 2, n2)
        swap.append(send(bundle(p, c), bundle(p, c), partner))
        t += small
        yield t
        for cp in swap:
            cp.wait_recv()
        done()

    pending = []
    state = {"w": 0}
    first = [True]

    def accumulate(block):
        q = wrap(z + block, nz)
        part = jnp.dot(
            hid[q], wts[lax.div(q, NX), lax.rem(q, NX)].reshape(cols, cols), preferred_element_type=F32
        )
        if first[0]:
            gin[...] = part
            first[0] = False
        else:
            gin[...] += part

    arrived = {}

    def block_here(block, parts):
        arrived[block] = arrived.get(block, 0) + parts
        if arrived[block] == CHUNKS:
            if state["w"] == 2:
                accumulate(block)
            else:
                pending.append(block)

    def w_done():
        state["w"] += 1
        if state["w"] == 2:
            for block in pending:
                accumulate(block)
            pending.clear()

    span = rows_blk // CHUNKS

    def hid_chunk(block, ch):
        return hid.at[wrap(z + block, nz), pl.ds(span * ch, span), :]

    def hid_ring(t0, step_time):
        flying = []
        for ch in range(CHUNKS):
            up_hops = nz // 2 if ch % 2 == 0 else nz // 2 - 1
            for sign, hops in ((1, up_hops), (-1, nz - 1 - up_hops)):
                cp = send(hid_chunk(0, ch), hid_chunk(0, ch), zdev(sign))
                flying.append([ch, sign, hops, 1, cp])
        block_here(0, CHUNKS)
        t = t0
        while flying:
            t += step_time
            yield t
            landed = []
            for item in list(flying):
                ch, sign, hops, k, cp = item
                cp.wait_recv()
                block = -sign * k
                landed.append(block % nz)
                if k < hops:
                    item[4] = send(hid_chunk(block, ch), hid_chunk(block, ch), zdev(sign))
                    item[3] = k + 1
                else:
                    flying.remove(item)
            for block in landed:
                block_here(block, 1)

    def tile_exchange(make_src, make_dst, toward):
        cps = []
        for i in range(1, nz // 2):
            j = jnp.where(c == 0, nz - i, i)
            cps.append(send(make_src(j), make_dst(j), (b, wrap(z + toward(j), nz))))
        half = nz // 2
        i = copy_count[0]
        copy_count[0] += 1
        last = pltpu.make_async_remote_copy(
            src_ref=make_src(half), dst_ref=make_dst(half), send_sem=send_sem.at[i], recv_sem=recv_sem.at[i],
            device_id=zdev(half), device_id_type=MESH_ID,
        )
        i = local_count[0]
        local_count[0] += 1
        own = pltpu.make_async_copy(make_src(0), make_dst(0), local_sem.at[i])

        @pl.when(c == 0)
        def _():
            last.start()

        @pl.when(c == 1)
        def _():
            own.start()

        def finish():
            for cp in cps:
                cp.wait_recv()

            @pl.when(c == 0)
            def _():
                last.wait()

            @pl.when(c == 1)
            def _():
                own.wait()

        return finish

    v_slices = t_slices(vals)
    tile_rows = lax.rem(y, 2) * NX + x

    def val_src(j):
        zd = wrap(z - j, nz)
        return val_in.at[pl.ds(mult(16 * tile_rows, 16), 16), pl.ds(mult(cols * zd + 128 * yhigh, 128), 128)]

    def val_dst(j):
        return vals.at[j, ylow, x, :, hi(y)]

    def both(make):
        parts = [make(half) for half in (0, 1)]
        live = list(parts)
        while live:
            due = None
            for part in list(live):
                try:
                    due = next(part)
                except StopIteration:
                    live.remove(part)
            if live:
                yield due

    def v_path():
        yield 0.01
        finish = tile_exchange(val_src, val_dst, lambda j: nz - j)
        yield 8.0
        finish()
        yield from both(lambda half: plane_gather(v_slices, half, 8.0, 2.2, 3.0, lambda: None))

    w_slices = (w_piece, w_row, w_col)
    run_streams(
        [
            hid_ring(0.0, 2.4),
            v_path(),
            both(lambda half: plane_gather(w_slices, half, 0.0, 2.3, 4.0, w_done)),
        ]
    )

    gate = gin[...]
    sig = jax.nn.sigmoid(gate)
    gate_value = gate * sig
    upstream = go[...].astype(F32)
    mg[...] = (upstream * gate_value).astype(BF)

    t_swap = []
    for owner in (oc, c):
        for jl in range(8):
            j = 8 * (1 - owner) + jl
            tterm[j] = jnp.dot(spread_t[j], mg[...], preferred_element_type=F32).astype(BF).reshape(2, NX, 16, cols)
        if not t_swap:
            t_swap = [send(tterm.at[jset(oc, h)], tr0.at[pl.ds(4 * h, 4)], partner) for h in (0, 1)]

    memory_read = jnp.dot(spread[...], vals[...].reshape(total_rows, cols), preferred_element_type=F32)
    bo_out[...] = (memory_read * gate_value).astype(BF)
    gg_f = (upstream * memory_read * (sig * (1.0 + gate * (1.0 - sig)))).astype(BF)
    gg[...] = gg_f
    ggt = gg_f.astype(F32).T.astype(BF)

    def make_iterm(block):
        q = wrap(z + block, nz)
        iterm[q] = lax.dot_general(
            gg[...], wts[lax.div(q, NX), lax.rem(q, NX)].reshape(cols, cols), NT, preferred_element_type=F32
        ).astype(BF)

    made = set()

    def need_iterm(block):
        if block % nz not in made:
            made.add(block % nz)
            make_iterm(block)

    def i_chunk(block, ch):
        return iterm.at[wrap(z + block, nz), pl.ds(span * ch, span), :]

    def hidden_ring(t0, step_time):
        flying = []
        for ch in range(CHUNKS):
            up_hops = nz // 2 if ch % 2 == 0 else nz // 2 - 1
            for sign, hops in ((1, up_hops), (-1, nz - 1 - up_hops)):
                need_iterm(sign * hops)
                slot = ri.at[(1 - sign) // 2, 0, pl.ds(span * ch, span), :]
                cp = send(i_chunk(sign * hops, ch), slot, zdev(sign))
                flying.append([ch, sign, hops, 1, cp])
        t = t0
        while flying:
            for item in flying:
                ch, sign, hops, k, cp = item
                if k < hops:
                    need_iterm(sign * (hops - k))
            t += step_time
            yield t
            for item in list(flying):
                ch, sign, hops, k, cp = item
                cp.wait_recv()
                if k < hops:
                    block = sign * (hops - k)
                    q = wrap(z + block, nz)
                    here = pl.ds(span * ch, span)
                    total = iterm[q, here, :].astype(F32) + ri[(1 - sign) // 2, k - 1, here, :].astype(F32)
                    iterm[q, here, :] = total.astype(BF)
                    slot = ri.at[(1 - sign) // 2, k, here, :]
                    item[4] = send(i_chunk(block, ch), slot, zdev(sign))
                    item[3] = k + 1
                else:
                    flying.remove(item)
        need_iterm(0)
        for ch in range(CHUNKS):
            up_hops = nz // 2 if ch % 2 == 0 else nz // 2 - 1
            here = pl.ds(span * ch, span)
            total = iterm[z, here, :].astype(F32)
            total = total + ri[0, up_hops - 1, here, :].astype(F32) + ri[1, nz - 2 - up_hops, here, :].astype(F32)
            gh_out[here, :] = total.astype(BF)

    def plane_reduce(slices, half, bufs, t0, small, large, finish):
        piece, row, col = slices
        rb, rp = bufs
        if half == 0:
            bundle = lambda p: row(p, half)
            line = lambda p: piece(y, p, half)
            pos, near, pos2, near2, n1, n2 = y, ydev, x, xdev, NY, NX
        else:
            bundle = lambda p: col(p, half)
            line = lambda p: piece(p, x, half)
            pos, near, pos2, near2, n1, n2 = x, xdev, y, ydev, NX, NY
        t = t0
        for stage, (at, p0, nr, n, rbuf, dt) in enumerate(
            ((bundle, pos, near, n1, rb, large), (line, pos2, near2, n2, rp, small))
        ):
            relay = send(at(wrap(p0 + 2, n)), rbuf.at[0], nr(s))
            direct = send(at(wrap(p0 - s, n)), rbuf.at[1], nr(-s))
            t += dt
            yield t
            relay.wait_recv()
            ahead = at(wrap(p0 + s, n))
            ahead[...] = (ahead[...].astype(F32) + rbuf[0].astype(F32)).astype(BF)
            comb = send(ahead, rbuf.at[2], nr(s))
            t += dt
            yield t
            direct.wait_recv()
            comb.wait_recv()
            mine = at(p0)
            total = mine[...].astype(F32) + rbuf[1].astype(F32) + rbuf[2].astype(F32)
            if stage == 0:
                mine[...] = total.astype(BF)
            else:
                finish(total)

    def ts_piece(yy, xx, half):
        return tsum.at[pl.ds(4 * half, 4), lax.rem(yy, 2), xx, :, hi(yy)]

    def ts_row(yy, half):
        return tsum.at[pl.ds(4 * half, 4), lax.rem(yy, 2), :, :, hi(yy)]

    def ts_col(xx, half):
        return tsum.at[pl.ds(4 * half, 4), :, xx]

    def g_src(j):
        jl = j - 8 * (1 - c)
        return tfin.at[jl]

    def g_src_fixed(j):
        return tfin.at[0] if isinstance(j, int) else g_src(j)

    def g_dst(j):
        return gvals.at[j, ylow, x, :, hi(y)]

    g_slices = t_slices(gvals)

    def t_half(half):
        yield 2.0
        t_swap[half].wait_recv()
        here = pl.ds(4 * half, 4)
        tsum[here] = (tterm[jset(c, half)].astype(F32) + tr0[here].astype(F32)).astype(BF)

        def finish(total):
            tfin[here] = total.astype(BF)

        yield from plane_reduce(
            (ts_piece, ts_row, ts_col), half, (tr_row if half == 0 else tr_col, tr_piece.at[half]),
            2.0, 2.2, 3.0, finish,
        )

    def t_path():
        yield from both(t_half)
        done = tile_exchange(g_src_fixed, g_dst, lambda j: j)
        yield 20.0
        done()
        yield from both(lambda half: plane_gather(g_slices, half, 20.0, 2.2, 3.0, lambda: None))
        for j in range(nz):
            q = wrap(z - j, nz)
            gv_out[:, pl.ds(mult(q * cols, cols), cols)] = gvals[j].reshape(rows_blk, cols).astype(F32)

    def ps_piece(yy, xx, half):
        return psum.at[yy, xx, pl.ds(128 * half, 128), :]

    def ps_row(yy, half):
        return psum.at[yy, :, pl.ds(128 * half, 128), :]

    def ps_col(xx, half):
        return psum.at[:, xx, pl.ds(128 * half, 128), :]

    def p_half(half):
        here = pl.ds(128 * half, 128)
        lhs = ggt[128 * half : 128 * half + 128, :]
        yield 0.5 + half
        for q in range(nz):
            pterm[q // NX, q % NX, here, :] = jnp.dot(lhs, hid[q], preferred_element_type=F32).astype(BF)
        swap = send(
            pterm.at[:, :, here, pl.ds(mult(128 * oc, 128), 128)], pr0.at[half], partner
        )
        yield 4.0 + half
        swap.wait_recv()
        own = pterm[:, :, here, pl.ds(mult(128 * c, 128), 128)]
        psum[:, :, here, :] = (own.astype(F32) + pr0[half].astype(F32)).astype(BF)

        def finish(total):
            gg_out[:, pl.ds(128 * half, 128)] = total.T

        yield from plane_reduce(
            (ps_piece, ps_row, ps_col), half, (pr_bundle.at[half], pr_piece.at[half]), 4.0 + half, 2.2, 4.5, finish
        )

    def aff_path():
        yield 3.0
        lane = jnp.bitwise_and(idx[...], 127)
        chunk = lax.shift_right_logical(idx[...], 7)
        acc = jnp.zeros((rows_blk, 128), F32)
        for j in range(nz):
            part = lax.dot_general(mg[...], vals[j].reshape(rows_blk, cols), NT, preferred_element_type=F32)
            got = jnp.take_along_axis(part, lane, axis=1, mode="promise_in_bounds")
            acc = jnp.where(chunk == j, got, acc)
        acc_t = acc.T
        for i in range(nz):
            affp[i] = acc_t[2 * i : 2 * i + 2, :]
        cps = [send(affp.at[wrap(z + k, nz)], affr.at[k], zdev(k)) for k in range(1, nz)]
        yield 13.0
        total = affp[z]
        for k in range(1, nz):
            cps[k - 1].wait_recv()
            total = total + affr[k]
        affall[z] = total
        cps = [send(affall.at[z], affall.at[z], zdev(k)) for k in range(1, nz)]
        yield 21.0
        for cp in cps:
            cp.wait_recv()
        for i in range(nz):
            afft[2 * i : 2 * i + 2, :] = affall[i]
        weights = wgt[...]
        aff = afft[...]
        pad_b[0:32, :] = weights * (aff - jnp.sum(weights * aff, axis=0, keepdims=True))
        gs_out[...] = pad_b[...].T[:, 0:32]

    run_streams([t_path(), hidden_ring(0.0, 2.5), p_half(0), p_half(1), aff_path()])

    for cp in sent:
        cp.wait_send()


def layer(nz, hidden_in, gate_weight, values, pick_rows, pick_scores, grad_out):
    rows, cols = hidden_in.shape
    vm = pltpu.VMEM
    scratch = [
        vm((nz, rows, cols), BF),
        vm((NY, NX, 2, rows, cols), BF),
        vm((nz, 2, NX, 16, cols), BF),
        vm((rows, nz * rows), BF),
        vm((nz, rows, rows), BF),
        vm((rows, cols), BF),
        vm((rows, cols), F32),
        vm((rows, cols), BF),
        vm((rows, cols), BF),
        vm((rows, 128), F32),
        vm((rows, 128), F32),
        vm((32, rows), jnp.int32),
        vm((32, rows), F32),
        vm((rows, 128), jnp.int32),
        vm((NY, NX, cols, cols), BF),
        vm((2, NY, NX, 128, 128), BF),
        vm((NY, NX, cols, 128), BF),
        vm((2, 3, 4, 128, 128), BF),
        vm((2, 3, 128, 128), BF),
        vm((nz, 2, NX, 16, cols), BF),
        vm((8, 2, NX, 16, cols), BF),
        vm((8, 2, NX, 16, cols), BF),
        vm((3, 4, NX, 16, 128), BF),
        vm((3, 4, 2, 16, cols), BF),
        vm((2, 3, 4, 16, 128), BF),
        vm((8, 16, 128), BF),
        vm((nz, 2, NX, 16, cols), BF),
        vm((nz, rows, cols), BF),
        vm((2, nz // 2, rows, cols), BF),
        vm((nz, 2, 128), F32),
        vm((nz, 2, 128), F32),
        vm((nz, 2, 128), F32),
        vm((32, 128), F32),
        pltpu.SemaphoreType.DMA((N_COPIES,)),
        pltpu.SemaphoreType.DMA((N_COPIES,)),
        pltpu.SemaphoreType.DMA((N_LOCAL,)),
    ]
    hbm = pl.BlockSpec(memory_space=pl.ANY)
    vmem = pl.BlockSpec(memory_space=pltpu.VMEM)
    return pl.pallas_call(
        functools.partial(body, nz),
        out_shape=(
            jax.ShapeDtypeStruct((rows, cols), BF),
            jax.ShapeDtypeStruct((rows, cols), BF),
            jax.ShapeDtypeStruct((rows, cols), F32),
            jax.ShapeDtypeStruct((rows, nz * cols), F32),
            jax.ShapeDtypeStruct((rows, 32), F32),
        ),
        in_specs=[hbm, hbm, hbm, vmem, vmem, hbm],
        out_specs=(vmem,) * 5,
        scratch_shapes=scratch,
        compiler_params=pltpu.CompilerParams(collective_id=0, has_side_effects=True),
    )(hidden_in, gate_weight, values, pick_rows, pick_scores, grad_out)


def solution(mesh):
    nz = mesh.shape["table"]
    return jax.shard_map(
        functools.partial(layer, nz),
        mesh=mesh,
        in_specs=(
            P("dp", "table"),
            P("dp", "table"),
            P("table", None),
            P("dp", None),
            P("dp", None),
            P("dp", "table"),
        ),
        out_specs=(
            P("dp", "table"),
            P("dp", "table"),
            P("dp", "table"),
            P("table", None),
            P("dp", None),
        ),
        check_vma=False,
    )
```

time: 571 us -> 109 us (0.19); the launches traced: 562 us -> 109 us
  waiting for transfers between devices: 411 us -> 0 us
  Pallas kernels: 0 us -> 96.2 us
  local copies, waits for them, and re-layouts: 62.3 us -> 12 us
  blocking collectives: 41.2 us -> 0 us
  starting transfers between devices: 16.1 us -> 0 us
  between operations: 14.3 us -> 0.64 us
  matrix products: 12 us -> 0 us
    all_gather x3 -> x0, waiting for transfers between devices: 128 us -> none  [the longest x1 67.3 us: local(): weight_full = lax.all_gather(gate_weight, 'dp', axis=0, tiled=True)]
    unnamed x7 -> x0, waiting for transfers between devices: 104 us -> none
    pallas_call x0 -> x1, Pallas kernels: none -> 96.2 us  [layer(): pl.pallas_call(functools.partial(body, nz), out_shape=(jax.ShapeDtypeStru...]
    psum x1 -> x0, waiting for transfers between devices: 66.9 us -> none  [local(): lax.psum(value_term.astype(jnp.bfloat16), 'dp').astype(jnp.float32)]
    reduce_scatter x1 -> x0, waiting for transfers between devices: 63.4 us -> none  [local(): lax.psum_scatter(input_term.astype(jnp.bfloat16), 'table', scatter_dimens...]
    all_to_all x1 -> x0, waiting for transfers between devices: 48.3 us -> none  [local(): lax.all_to_all(partial_mem.astype(jnp.bfloat16), 'table', split_axis=1, c...]
    psum x1 -> x0, blocking collectives: 41.2 us -> none  [local(): affinity = lax.psum(affinity_part, 'table')]
    gather x3 -> x0, local copies, waits for them, and re-layouts: 25.8 us -> none  [local(): jnp.take_along_axis(affinity_all, jnp.where(owned, local_rows, 0), axis=1)]
  transfers between devices with their start and end apart: 7 -> 0, of which waited for: 7 -> 0; matrix products, arithmetic and copies ran while one was open for 13% -> 0% of each run, Pallas kernels for 0% -> 0%
where the time goes in v1:
time: 109 us
  Pallas kernels  96.2 us (88%)
  local copies, waits for them, and re-layouts  12 us (11%)
    pallas_call x1, Pallas kernels, layer(): pl.pallas_call(functools.partial(body, nz), out_shape=(jax.ShapeDtypeStru...  96.2 us
    unnamed x6, local copies, waits for them, and re-layouts  10.5 us

profile of v1, /device:TPU:1, one launch (start us, length us, event | category | flops | bytes accessed | tf_op | source)
XLA Modules:
  0.0 108.9 jit_solution(1435534753216775352)
XLA Ops:
  0.6 1.4 %copy.11.rows_in = s32[128,32]{1,0:T(8,128)} copy(s32[128,32]{0,1:T(8,128)} %param.9) | data formatting | bytes 32768 | tf_op args[3]
  2.1 1.4 %copy.12.score_in = f32[128,32]{1,0:T(8,128)} copy(f32[128,32]{0,1:T(8,128)} %param.10) | data formatting | bytes 32768 | tf_op args[4]
  3.5 96.2 %shard_map.101 = (bf16[128,256]{1,0:T(8,128)(2,1)}, bf16[128,256]{1,0:T(8,128)(2,1)}, f32[128,256]{1,0:T(8,128)}, f32[128,4096]{1,0:T(8,128)}, f32[128,32]{1,0:T(8,128)}) custom-call(bf16[128,256]{1,0:T(8,128)(2,1)} %hid_in.1, bf16[128,256]{1,0:T(8,128)(2,1)} %w_in.1, bf16[128,4096]{1,0:T(8,128)(2,1)} %val_in.1, s32[128,32]{1,0:T(8,128)} %copy.11.rows_in, ...), custom_call_target="tpu_custom_call" | custom-call | tf_op jit(solution)/shard_map/pallas_call | solution.py:620
  99.7 1.5 %copy.13 = f32[128,32]{0,1:T(8,128)} copy(f32[128,32]{1,0:T(8,128)} %get-tuple-element.9) | data formatting | bytes 32768 | tf_op jit(solution)/shard_map/pallas_call | solution.py:620
  101.3 1.5 %copy.18 = bf16[128,256]{1,0:T(8,128)(2,1)} copy(bf16[128,256]{1,0:T(8,128)(2,1)} %get-tuple-element.15) | data formatting | bytes 131072
  102.7 1.5 %copy.19 = bf16[128,256]{1,0:T(8,128)(2,1)} copy(bf16[128,256]{1,0:T(8,128)(2,1)} %get-tuple-element.16) | data formatting | bytes 131072
  104.2 1.6 %copy.20 = f32[128,256]{1,0:T(8,128)} copy(f32[128,256]{1,0:T(8,128)} %get-tuple-element.17) | data formatting | bytes 262144
  105.8 3.1 %copy.21 = f32[128,4096]{1,0:T(8,128)} copy(f32[128,4096]{1,0:T(8,128)} %get-tuple-element.18) | data formatting | bytes 4194304

commit v2 on v1

v2 whole, which is shorter than its diff:
```python
import functools
import heapq

import jax
import jax.numpy as jnp
from jax import lax
from jax.experimental import pallas as pl
from jax.experimental.pallas import tpu as pltpu
from jax.sharding import PartitionSpec as P

MESH_ID = pl.DeviceIdType.MESH
F32 = jnp.float32
BF = jnp.bfloat16
NX = 4
NY = 4
CHUNKS = 2
N_COPIES = 256
N_LOCAL = 16
NT = (((1,), (1,)), ((), ()))


def wrap(value, size):
    return lax.rem(value + size, size)


def mult(value, unit):
    return pl.multiple_of(value, unit)


def run_streams(streams):
    heap = []
    for order, stream in enumerate(streams):
        heapq.heappush(heap, (0.0, order, stream))
    while heap:
        when, order, stream = heapq.heappop(heap)
        try:
            due = next(stream)
        except StopIteration:
            continue
        heapq.heappush(heap, (due, order, stream))


def body(
    nz,
    hid_in, w_in, val_in, rows_in, score_in, go_in,
    bo_out, gh_out, gg_out, gvals_out, gs_out,
    hid, wts, vals, spread, spread_t, go, gin, mg, gg, ggt, pad_a, picks, rel_t, wgt, idx,
    pterm, pr0, psum, pr_bundle, pr_piece,
    tterm, tr0, tsum, tr_row, tr_col, tr_piece, tfin, gvals,
    iterm, ri_even, ri_odd, affp, affr, affall, afft,
    send_sem, recv_sem, local_sem, know,
):
    rows_blk = hid_in.shape[0]
    cols = hid_in.shape[1]
    b = lax.axis_index("dp")
    z = lax.axis_index("table")
    c = lax.rem(b, 2)
    x = lax.rem(lax.div(b, 2), NX)
    y = lax.div(b, 2 * NX)
    s = 1 - 2 * c
    oc = 1 - c

    def dev(yy, xx, cc):
        return ((yy * NX + xx) * 2 + cc, z)

    def zdev(delta):
        return (b, wrap(z + delta, nz))

    def xdev(delta):
        return dev(y, wrap(x + delta, NX), c)

    def ydev(delta):
        return dev(wrap(y + delta, NY), x, c)

    partner = dev(y, x, oc)

    barrier = pltpu.get_barrier_semaphore()
    peers = [zdev(k) for k in (1, -1, 2, -2)] + [xdev(k) for k in (1, 2, 3)] + [ydev(k) for k in (1, 2, 3)]
    peers.append(partner)
    for peer in peers:
        pl.semaphore_signal(barrier, inc=1, device_id=peer, device_id_type=MESH_ID)

    local_count = [0]
    copy_count = [0]
    sent = []

    def lcopy(src, dst):
        i = local_count[0]
        local_count[0] += 1
        cp = pltpu.make_async_copy(src, dst, local_sem.at[i])
        cp.start()
        return cp

    def send(src, dst, peer):
        i = copy_count[0]
        copy_count[0] += 1
        cp = pltpu.make_async_remote_copy(
            src_ref=src, dst_ref=dst, send_sem=send_sem.at[i], recv_sem=recv_sem.at[i],
            device_id=peer, device_id_type=MESH_ID,
        )
        cp.start()
        sent.append(cp)
        return cp

    own_rows = lcopy(rows_in, picks)
    own_scores = lcopy(score_in, wgt)
    own_w = lcopy(w_in, wts.at[y, x, c])
    own_h = lcopy(hid_in, hid.at[z])
    own_g = lcopy(go_in, go)

    ylow = lax.rem(y, 2)
    yhigh = lax.div(y, 2)

    pad_a[...] = jnp.zeros_like(pad_a)
    own_rows.wait()
    own_scores.wait()
    pad_a[0:32, :] = picks[...].astype(F32)
    total_rows = nz * rows_blk

    def relative(row_f):
        shifted = row_f.astype(jnp.int32) + (total_rows - rows_blk * z)
        return jnp.where(shifted >= total_rows, shifted - total_rows, shifted)

    idx[...] = relative(pad_a[...].T)
    rel_t[...] = relative(pad_a[0:32, :])
    scores = wgt[...]
    expo = jnp.exp(scores - jnp.max(scores, axis=0, keepdims=True))
    wgt[...] = expo / jnp.sum(expo, axis=0, keepdims=True)
    weights_bf = wgt[...].astype(BF).astype(F32)
    afft[...] = weights_bf

    def spread_block(i, carry):
        ids = lax.broadcasted_iota(jnp.int32, (rows_blk, rows_blk), 0) + i * rows_blk
        acc = jnp.zeros((rows_blk, rows_blk), F32)
        for k in range(32):
            acc = jnp.where(rel_t[k : k + 1, :] == ids, afft[k : k + 1, :], acc)
        spread_t[i] = acc.astype(BF)
        spread[:, pl.ds(mult(i * rows_blk, rows_blk), rows_blk)] = acc.T.astype(BF)
        return carry

    own_w.wait()
    own_h.wait()
    own_g.wait()
    pl.semaphore_wait(barrier, len(peers))

    def w_piece(yy, xx, cc, half):
        return wts.at[yy, xx, cc, :, pl.ds(128 * half, 128)]

    def w_row(yy, cc, half):
        return wts.at[yy, :, cc, :, pl.ds(128 * half, 128)]

    def w_col(xx, cc, half):
        return wts.at[:, xx, cc, :, pl.ds(128 * half, 128)]

    def jset(cc, half):
        return pl.ds(8 * (1 - cc) + 4 * half, 4)

    def hi(yy):
        return pl.ds(mult(128 * lax.div(yy, 2), 128), 128)

    def t_slices(buf):
        def piece(yy, xx, cc, half):
            return buf.at[jset(cc, half), lax.rem(yy, 2), xx, :, hi(yy)]

        def row(yy, cc, half):
            return buf.at[jset(cc, half), lax.rem(yy, 2), :, :, hi(yy)]

        def col(xx, cc, half):
            return buf.at[jset(cc, half), :, xx]

        return piece, row, col

    flags = set()

    def until(name, t):
        while name not in flags:
            yield t
            t += 0.5

    def both(make):
        live = [make(half) for half in (0, 1)]
        while live:
            due = None
            for part in list(live):
                try:
                    due = next(part)
                except StopIteration:
                    live.remove(part)
            if live:
                yield due

    def plane_gather(slices, half, t, first_step, second_step, third_step):
        piece, row, col = slices
        if half == 0:
            line = lambda p: piece(y, p, c, half)
            bundle = lambda p: row(p, c, half)
            pos, near, pos2, near2, n1, n2 = x, xdev, y, ydev, NX, NY
        else:
            line = lambda p: piece(p, x, c, half)
            bundle = lambda p: col(p, c, half)
            pos, near, pos2, near2, n1, n2 = y, ydev, x, xdev, NY, NX
        out = [send(line(pos), line(pos), near(k)) for k in (2, 1, 3)]
        t += first_step
        yield t
        for cp in out:
            cp.wait_recv()
        out = [send(bundle(pos2), bundle(pos2), near2(k)) for k in (2, 1, 3)]
        swap = [send(bundle(pos2), bundle(pos2), partner)]
        t += second_step
        yield t
        for k, cp in ((1, out[1]), (3, out[2]), (2, out[0])):
            cp.wait_recv()
            p = wrap(pos2 - k, n2)
            swap.append(send(bundle(p), bundle(p), partner))
        t += third_step
        yield t
        for cp in swap:
            cp.wait_recv()

    pending = []
    first = [True]

    def accumulate(block):
        q = wrap(z + block, nz)
        part = jnp.dot(
            hid[q], wts[lax.div(q, NX), lax.rem(q, NX)].reshape(cols, cols), preferred_element_type=F32
        )
        if first[0]:
            gin[...] = part
            first[0] = False
        else:
            gin[...] += part

    arrived = {}

    def block_here(block, parts):
        arrived[block] = arrived.get(block, 0) + parts
        if arrived[block] == CHUNKS:
            if "w" in flags:
                accumulate(block)
            else:
                pending.append(block)

    span = rows_blk // CHUNKS

    def hid_chunk(block, ch):
        return hid.at[wrap(z + block, nz), pl.ds(span * ch, span), :]

    def limits(ch):
        up = nz // 2 if ch % 2 == 0 else nz // 2 - 1
        return ((1, up), (-1, nz - 1 - up))

    def hid_relay(t, step_time):
        def pass_on(ch, sign, limit, k):
            at = hid_chunk(-sign * k, ch)
            far = send(at, at, zdev(2 * sign)) if k + 2 <= limit else None
            near = send(at, at, zdev(sign)) if k + 1 <= limit else None
            return [ch, sign, limit, k, near, far]

        flying = [pass_on(ch, sign, limit, 0) for ch in range(CHUNKS) for sign, limit in limits(ch)]
        block_here(0, CHUNKS)
        lax.fori_loop(0, nz, spread_block, 0)
        while flying:
            t += step_time
            yield t
            following, landed = [], []
            for ch, sign, limit, k, near, far in flying:
                if far is not None:
                    far.wait_recv()
                    following.append(pass_on(ch, sign, limit, k + 2))
                    landed.append((-sign * (k + 2)) % nz)
                if near is not None:
                    near.wait_recv()
                    landed.append((-sign * (k + 1)) % nz)
            flying = following
            for block in landed:
                block_here(block, 1)
        yield from until("w", t)
        flags.add("h")

    def tile_exchange(make_src, make_dst, toward):
        cps = []
        for i in range(1, nz // 2):
            j = jnp.where(c == 0, nz - i, i)
            cps.append(send(make_src(j), make_dst(j), (b, wrap(z + toward(j), nz))))
        half = nz // 2
        i = copy_count[0]
        copy_count[0] += 1
        last = pltpu.make_async_remote_copy(
            src_ref=make_src(half), dst_ref=make_dst(half), send_sem=send_sem.at[i], recv_sem=recv_sem.at[i],
            device_id=zdev(half), device_id_type=MESH_ID,
        )
        i = local_count[0]
        local_count[0] += 1
        own = pltpu.make_async_copy(make_src(0), make_dst(0), local_sem.at[i])

        @pl.when(c == 0)
        def _():
            last.start()

        @pl.when(c == 1)
        def _():
            own.start()

        def finish():
            for cp in cps:
                cp.wait_recv()

            @pl.when(c == 0)
            def _():
                last.wait()

            @pl.when(c == 1)
            def _():
                own.wait()

        return finish

    v_slices = t_slices(vals)
    tile_rows = lax.rem(y, 2) * NX + x

    def val_src(j):
        zd = wrap(z - j, nz)
        return val_in.at[pl.ds(mult(16 * tile_rows, 16), 16), pl.ds(mult(cols * zd + 128 * yhigh, 128), 128)]

    def val_dst(j):
        return vals.at[j, ylow, x, :, hi(y)]

    def both(make):
        parts = [make(half) for half in (0, 1)]
        live = list(parts)
        while live:
            due = None
            for part in list(live):
                try:
                    due = next(part)
                except StopIteration:
                    live.remove(part)
            if live:
                yield due

    def v_path():
        yield 0.0
        for stage, reach in enumerate((2, 4)):
            for sign in (1, -1):
                pl.semaphore_signal(know.at[stage], inc=1, device_id=zdev(sign * reach), device_id_type=MESH_ID)
            yield (1.6, 4.5)[stage]
            pl.semaphore_wait(know.at[stage], 2)
        finish = tile_exchange(val_src, val_dst, lambda j: nz - j)
        yield 12.5
        finish()
        yield from both(lambda half: plane_gather(v_slices, half, 12.5, 3.4, 5.5, 1.5))
        flags.add("v")

    w_slices = (w_piece, w_row, w_col)

    def w_path():
        yield from both(lambda half: plane_gather(w_slices, half, 0.0, 3.5, 8.0, 1.7))
        flags.add("w")
        for block in pending:
            accumulate(block)
        pending.clear()

    def gate_parts():
        gate = gin[...]
        sig = jax.nn.sigmoid(gate)
        return gate, sig, go[...].astype(F32)

    t_swap = []

    def value_terms():
        gate, sig, upstream = gate_parts()
        mg[...] = (upstream * (gate * sig)).astype(BF)
        for owner in (oc, c):
            for jl in range(8):
                j = 8 * (1 - owner) + jl
                tterm[j] = (
                    jnp.dot(spread_t[j], mg[...], preferred_element_type=F32).astype(BF).reshape(2, NX, 16, cols)
                )
            if not t_swap:
                t_swap.extend(send(tterm.at[jset(oc, h)], tr0.at[pl.ds(4 * h, 4)], partner) for h in (0, 1))

    def gate_gradient():
        gate, sig, upstream = gate_parts()
        memory_read = jnp.dot(spread[...], vals[...].reshape(total_rows, cols), preferred_element_type=F32)
        bo_out[...] = (memory_read * (gate * sig)).astype(BF)
        slope = (upstream * memory_read * (sig * (1.0 + gate * (1.0 - sig)))).astype(BF)
        gg[...] = slope
        ggt[...] = slope.astype(F32).T.astype(BF)

    def make_iterm(block):
        q = wrap(z + block, nz)
        iterm[q] = lax.dot_general(
            gg[...], wts[lax.div(q, NX), lax.rem(q, NX)].reshape(cols, cols), NT, preferred_element_type=F32
        ).astype(BF)

    made = set()

    def need_iterm(block):
        if block % nz not in made:
            made.add(block % nz)
            make_iterm(block)

    def i_chunk(block, ch):
        return iterm.at[wrap(z + block, nz), pl.ds(span * ch, span), :]

    def slots(buf, sign, at, ch):
        return buf.at[(1 - sign) // 2, at, pl.ds(span * ch, span), :]

    def hidden_relay(t, step_time):
        yield from until("v", t)
        gate_gradient()
        flags.add("g")
        todo = [(ch, sign, limit) for ch in range(CHUNKS) for sign, limit in limits(ch)]
        far, near = {}, {}

        def start(ch, sign, dist, step):
            need_iterm(sign * dist)
            cps, buf = (far, ri_even) if step == 2 else (near, ri_odd)
            cps[ch, sign] = send(i_chunk(sign * dist, ch), slots(buf, sign, (dist - 1) // 2, ch), zdev(step * sign))

        for ch, sign, limit in todo:
            if limit == 8:
                start(ch, sign, 8, 2)
            start(ch, sign, 7, 1)
        for dist in (6, 4, 2, 0):
            for ch, sign, limit in todo:
                need_iterm(sign * dist)
                if dist:
                    need_iterm(sign * (dist - 1))
            t += step_time
            yield t
            for ch, sign, limit in todo:
                here = pl.ds(span * ch, span)
                side = (1 - sign) // 2
                q = wrap(z + sign * dist, nz)
                total = iterm[q, here, :].astype(F32)
                if (ch, sign) in far:
                    far[ch, sign].wait_recv()
                    total = total + ri_even[side, (dist + 1) // 2, here, :].astype(F32)
                near[ch, sign].wait_recv()
                total = total + ri_odd[side, dist // 2, here, :].astype(F32)
                if dist:
                    iterm[q, here, :] = total.astype(BF)
                    start(ch, sign, dist, 2)
                    start(ch, sign, dist - 1, 1)
                elif sign == limits(ch)[0][0]:
                    held = total
                    gin[here, :] = held
                else:
                    total = total - iterm[q, here, :].astype(F32) + gin[here, :]
                    gh_out[here, :] = total.astype(BF)

    def plane_reduce(slices, half, bufs, t, small, large, finish):
        piece, row, col = slices
        rb, rp = bufs
        if half == 0:
            bundle = lambda p: row(p, half)
            line = lambda p: piece(y, p, half)
            pos, near, pos2, near2, n1, n2 = y, ydev, x, xdev, NY, NX
        else:
            bundle = lambda p: col(p, half)
            line = lambda p: piece(p, x, half)
            pos, near, pos2, near2, n1, n2 = x, xdev, y, ydev, NX, NY
        for stage, (at, p0, nr, n, rbuf, dt) in enumerate(
            ((bundle, pos, near, n1, rb, large), (line, pos2, near2, n2, rp, small))
        ):
            out = [send(at(wrap(p0 + k, n)), rbuf.at[k - 1], nr(k)) for k in (2, 1, 3)]
            t += dt
            yield t
            for cp in out:
                cp.wait_recv()
            mine = at(p0)
            total = mine[...].astype(F32)
            for k in range(3):
                total = total + rbuf[k].astype(F32)
            if stage == 0:
                mine[...] = total.astype(BF)
            else:
                finish(total)

    def ts_piece(yy, xx, half):
        return tsum.at[pl.ds(4 * half, 4), lax.rem(yy, 2), xx, :, hi(yy)]

    def ts_row(yy, half):
        return tsum.at[pl.ds(4 * half, 4), lax.rem(yy, 2), :, :, hi(yy)]

    def ts_col(xx, half):
        return tsum.at[pl.ds(4 * half, 4), :, xx]

    def g_src(j):
        jl = j - 8 * (1 - c)
        return tfin.at[jl]

    def g_src_fixed(j):
        return tfin.at[0] if isinstance(j, int) else g_src(j)

    def g_dst(j):
        return gvals.at[j, ylow, x, :, hi(y)]

    g_slices = t_slices(gvals)

    def t_half(half):
        yield 20.5
        t_swap[half].wait_recv()
        here = pl.ds(4 * half, 4)
        tsum[here] = (tterm[jset(c, half)].astype(F32) + tr0[here].astype(F32)).astype(BF)

        def finish(total):
            tfin[here] = total.astype(BF)

        yield from plane_reduce(
            (ts_piece, ts_row, ts_col), half, (tr_row if half == 0 else tr_col, tr_piece.at[half]),
            20.5, 3.6, 5.6, finish,
        )

    def t_path():
        yield from until("h", 18.0)
        value_terms()
        yield from both(t_half)
        done = tile_exchange(g_src_fixed, g_dst, lambda j: j)
        yield 37.5
        done()
        yield from both(lambda half: plane_gather(g_slices, half, 37.5, 3.4, 5.5, 1.5))
        gvals_out[...] = gvals[...]

    def ps_piece(yy, xx, half):
        return psum.at[yy, xx, pl.ds(128 * half, 128), :]

    def ps_row(yy, half):
        return psum.at[yy, :, pl.ds(128 * half, 128), :]

    def ps_col(xx, half):
        return psum.at[:, xx, pl.ds(128 * half, 128), :]

    def p_half(half):
        here = pl.ds(128 * half, 128)
        yield from until("g", 24.5 + half)
        yield 25.0 + half
        for q in range(nz):
            pterm[q // NX, q % NX, here, :] = jnp.dot(ggt[here, :], hid[q], preferred_element_type=F32).astype(BF)
        swap = send(
            pterm.at[:, :, here, pl.ds(mult(128 * oc, 128), 128)], pr0.at[half], partner
        )
        yield 28.0 + half
        swap.wait_recv()
        own = pterm[:, :, here, pl.ds(mult(128 * c, 128), 128)]
        psum[:, :, here, :] = (own.astype(F32) + pr0[half].astype(F32)).astype(BF)

        def finish(total):
            gg_out[:, pl.ds(128 * half, 128)] = total.T

        yield from plane_reduce(
            (ps_piece, ps_row, ps_col), half, (pr_bundle.at[half], pr_piece.at[half]), 28.0 + half, 4.3, 8.3, finish
        )

    def aff_path():
        yield from until("g", 25.0)
        yield 26.5
        lane = jnp.bitwise_and(idx[...], 127)
        chunk = lax.shift_right_logical(idx[...], 7)
        acc = jnp.zeros((rows_blk, 128), F32)
        for j in range(nz):
            part = lax.dot_general(mg[...], vals[j].reshape(rows_blk, cols), NT, preferred_element_type=F32)
            got = jnp.take_along_axis(part, lane, axis=1, mode="promise_in_bounds")
            acc = jnp.where(chunk == j, got, acc)
        acc_t = acc.T
        for i in range(nz):
            affp[i] = acc_t[2 * i : 2 * i + 2, :]
        cps = [send(affp.at[wrap(z + k, nz)], affr.at[k], zdev(k)) for k in range(1, nz)]
        yield 35.0
        total = affp[z]
        for k in range(1, nz):
            cps[k - 1].wait_recv()
            total = total + affr[k]
        affall[z] = total
        cps = [send(affall.at[z], affall.at[z], zdev(k)) for k in range(1, nz)]
        yield 43.0
        for cp in cps:
            cp.wait_recv()
        for i in range(nz):
            afft[2 * i : 2 * i + 2, :] = affall[i]
        weights = wgt[...]
        aff = afft[...]
        gs_out[...] = weights * (aff - jnp.sum(weights * aff, axis=0, keepdims=True))

    run_streams(
        [hid_relay(0.0, 4.0), w_path(), v_path(), t_path(), hidden_relay(23.0, 4.0), p_half(0), p_half(1), aff_path()]
    )

    for cp in sent:
        cp.wait_send()


def write_out(nz, bo_in, gh_in, gg_in, gvals_in, gs_in, bo_out, gh_out, gg_out, gv_out, gs_out, wide, sem):
    rows, cols = bo_in.shape
    z = lax.axis_index("table")
    small = ((bo_in, bo_out), (gh_in, gh_out), (gg_in, gg_out), (gs_in, gs_out))
    copies = [pltpu.make_async_copy(src, dst, sem.at[nz + i]) for i, (src, dst) in enumerate(small)]
    for cp in copies:
        cp.start()
    for j in range(nz):
        wide[j] = gvals_in[j].reshape(rows, cols).astype(F32)
        q = wrap(z - j, nz)
        cp = pltpu.make_async_copy(wide.at[j], gv_out.at[:, pl.ds(mult(q * cols, cols), cols)], sem.at[j])
        cp.start()
        copies.append(cp)
    for cp in copies:
        cp.wait()


def layer(nz, hidden_in, gate_weight, values, pick_rows, pick_scores, grad_out):
    rows, cols = hidden_in.shape
    vm = pltpu.VMEM
    scratch = [
        vm((nz, rows, cols), BF),
        vm((NY, NX, 2, rows, cols), BF),
        vm((nz, 2, NX, 16, cols), BF),
        vm((rows, nz * rows), BF),
        vm((nz, rows, rows), BF),
        vm((rows, cols), BF),
        vm((rows, cols), F32),
        vm((rows, cols), BF),
        vm((rows, cols), BF),
        vm((cols, rows), BF),
        vm((rows, 128), F32),
        vm((32, rows), jnp.int32),
        vm((32, rows), jnp.int32),
        vm((32, rows), F32),
        vm((rows, 128), jnp.int32),
        vm((NY, NX, cols, cols), BF),
        vm((2, NY, NX, 128, 128), BF),
        vm((NY, NX, cols, 128), BF),
        vm((2, 3, 4, 128, 128), BF),
        vm((2, 3, 128, 128), BF),
        vm((nz, 2, NX, 16, cols), BF),
        vm((8, 2, NX, 16, cols), BF),
        vm((8, 2, NX, 16, cols), BF),
        vm((3, 4, NX, 16, 128), BF),
        vm((3, 4, 2, 16, cols), BF),
        vm((2, 3, 4, 16, 128), BF),
        vm((8, 16, 128), BF),
        vm((nz, 2, NX, 16, cols), BF),
        vm((nz, rows, cols), BF),
        vm((2, nz // 4, rows, cols), BF),
        vm((2, nz // 4, rows, cols), BF),
        vm((nz, 2, 128), F32),
        vm((nz, 2, 128), F32),
        vm((nz, 2, 128), F32),
        vm((32, 128), F32),
        pltpu.SemaphoreType.DMA((N_COPIES,)),
        pltpu.SemaphoreType.DMA((N_COPIES,)),
        pltpu.SemaphoreType.DMA((N_LOCAL,)),
        pltpu.SemaphoreType.REGULAR((2,)),
    ]
    hbm = pl.BlockSpec(memory_space=pl.ANY)
    vmem = pl.BlockSpec(memory_space=pltpu.VMEM)
    arrays = (hidden_in, gate_weight, values, pick_rows.T, pick_scores.T, grad_out)
    arrays = [pltpu.with_memory_space_constraint(a, pltpu.HBM) for a in arrays]
    parts = pl.pallas_call(
        functools.partial(body, nz),
        out_shape=(
            jax.ShapeDtypeStruct((rows, cols), BF),
            jax.ShapeDtypeStruct((rows, cols), BF),
            jax.ShapeDtypeStruct((rows, cols), F32),
            jax.ShapeDtypeStruct((nz, 2, NX, 16, cols), BF),
            jax.ShapeDtypeStruct((32, rows), F32),
        ),
        in_specs=[pl.BlockSpec(memory_space=pltpu.HBM)] * 6,
        out_specs=(vmem,) * 5,
        scratch_shapes=scratch,
        compiler_params=pltpu.CompilerParams(
            collective_id=0, has_side_effects=True, vmem_limit_bytes=32 * 1024 * 1024
        ),
    )(*arrays)
    bo, gh, gg, gv, gs = pl.pallas_call(
        functools.partial(write_out, nz),
        out_shape=(
            jax.ShapeDtypeStruct((rows, cols), BF),
            jax.ShapeDtypeStruct((rows, cols), BF),
            jax.ShapeDtypeStruct((rows, cols), F32),
            jax.ShapeDtypeStruct((rows, nz * cols), F32),
            jax.ShapeDtypeStruct((32, rows), F32),
        ),
        in_specs=[vmem] * 5,
        out_specs=(hbm,) * 5,
        scratch_shapes=[pltpu.VMEM((nz, rows, cols), F32), pltpu.SemaphoreType.DMA((nz + 4,))],
        compiler_params=pltpu.CompilerParams(vmem_limit_bytes=8 * 1024 * 1024),
    )(*parts)
    return bo, gh, gg, gv, gs.T


def solution(mesh):
    nz = mesh.shape["table"]
    return jax.shard_map(
        functools.partial(layer, nz),
        mesh=mesh,
        in_specs=(
            P("dp", "table"),
            P("dp", "table"),
            P("table", None),
            P("dp", None),
            P("dp", None),
            P("dp", "table"),
        ),
        out_specs=(
            P("dp", "table"),
            P("dp", "table"),
            P("dp", "table"),
            P("table", None),
            P("dp", None),
        ),
        check_vma=False,
    )
```

time: 109 us -> 80 us (0.73)
  Pallas kernels: 96.2 us -> 79.2 us
  local copies, waits for them, and re-layouts: 12 us -> 0 us
    pallas_call x1, Pallas kernels: 96.2 us -> 77.6 us  [layer(): pl.pallas_call(functools.partial(body, nz), out_shape=(jax.ShapeDtypeStru...]
    unnamed x6 -> x0, local copies, waits for them, and re-layouts: 10.5 us -> none
    pallas_call x0 -> x1, Pallas kernels: none -> 1.57 us  [layer(): pl.pallas_call(functools.partial(write_out, nz), out_shape=(jax.ShapeDtyp...]
    pallas_call x1 -> x0, local copies, waits for them, and re-layouts: 1.52 us -> none  [layer(): pl.pallas_call(functools.partial(body, nz), out_shape=(jax.ShapeDtypeStru...]
where the time goes in v2:
time: 80 us; the launch traced here: 79.8 us
  Pallas kernels  79.2 us (99%)
    pallas_call x1, Pallas kernels, layer(): pl.pallas_call(functools.partial(body, nz), out_shape=(jax.ShapeDtypeStru...  77.6 us

profile of v2, /device:TPU:1, one launch (start us, length us, event | category | flops | bytes accessed | tf_op | source)
XLA Modules:
  0.0 79.8 jit_solution(15859220290344460675)
XLA Ops:
  0.6 77.6 %shard_map.101 = (bf16[128,256]{1,0:T(8,128)(2,1)S(1)}, bf16[128,256]{1,0:T(8,128)(2,1)S(1)}, f32[128,256]{1,0:T(8,128)S(1)}, bf16[16,2,4,16,256]{4,3,2,1,0:T(8,128)(2,1)S(1)}, f32[32,128]{1,0:T(8,128)S(1)}) custom-call(bf16[128,256]{1,0:T(8,128)(2,1)} %hid_in.1, bf16[128,256]{1,0:T(8,128)(2,1)} %w_in.1, bf16[128,4096]{1,0:T(8,128)(2,1)} %val_in.1, ...), custom_call_target="tpu_custom_call" | custom-call | tf_op jit(solution)/shard_map/pallas_call | solution.py:660
  78.3 1.6 %shard_map.102 = (bf16[128,256]{1,0:T(8,128)(2,1)}, bf16[128,256]{1,0:T(8,128)(2,1)}, f32[128,256]{1,0:T(8,128)}, f32[128,4096]{1,0:T(8,128)}, f32[32,128]{1,0:T(8,128)}) custom-call(bf16[128,256]{1,0:T(8,128)(2,1)S(1)} %get-tuple-element.15.bo_in, bf16[128,256]{1,0:T(8,128)(2,1)S(1)} %get-tuple-element.16.gh_in, f32[128,256]{1,0:T(8,128)S(1)} %get-tuple-element.17.gg_in, ...), custom_call_target="tpu_custom_call" | custom-call | tf_op jit(solution)/shard_map/pallas_call | solution.py:676

commit v3 on v2

--- a/solution.py
+++ b/solution.py
@@ -13,10 +13,20 @@
 BF = jnp.bfloat16
 NX = 4
 NY = 4
-CHUNKS = 2
-N_COPIES = 256
+CHUNKS = 4
+N_COPIES = 320
 N_LOCAL = 16
 NT = (((1,), (1,)), ((), ()))
+RELAY = {1: 0, 2: 0, 3: 2, 4: 2, 5: 4, 6: 4, 7: 6, 8: 6}
+RING = {k: k - 1 for k in range(1, 9)}
+
+
+def hop_time(links):
+    return 3.4 + 1.0 * (links - 1)
+
+
+def children_of(parents, node, limit):
+    return sorted((k for k, p in parents.items() if p == node and k <= limit), reverse=True)
 
 
 def wrap(value, size):
@@ -43,11 +53,11 @@
 def body(
     nz,
     hid_in, w_in, val_in, rows_in, score_in, go_in,
-    bo_out, gh_out, gg_out, gvals_out, gs_out,
+    bo_out, gh_out, gg_out, gvals, gs_out,
     hid, wts, vals, spread, spread_t, go, gin, mg, gg, ggt, pad_a, picks, rel_t, wgt, idx,
     pterm, pr0, psum, pr_bundle, pr_piece,
-    tterm, tr0, tsum, tr_row, tr_col, tr_piece, tfin, gvals,
-    iterm, ri_even, ri_odd, affp, affr, affall, afft,
+    tterm, tr0, tsum, tr_row, tr_col, tr_piece, tfin,
+    iterm, ri, affp, affr, affall, afft,
     send_sem, recv_sem, local_sem, know,
 ):
     rows_blk = hid_in.shape[0]
@@ -250,32 +260,27 @@
         up = nz // 2 if ch % 2 == 0 else nz // 2 - 1
         return ((1, up), (-1, nz - 1 - up))
 
-    def hid_relay(t, step_time):
-        def pass_on(ch, sign, limit, k):
+    def hid_relay(t):
+        waiting = []
+
+        def pass_on(ch, sign, limit, k, now):
             at = hid_chunk(-sign * k, ch)
-            far = send(at, at, zdev(2 * sign)) if k + 2 <= limit else None
-            near = send(at, at, zdev(sign)) if k + 1 <= limit else None
-            return [ch, sign, limit, k, near, far]
-
-        flying = [pass_on(ch, sign, limit, 0) for ch in range(CHUNKS) for sign, limit in limits(ch)]
+            for child in children_of(RELAY, k, limit):
+                cp = send(at, at, zdev(sign * (child - k)))
+                leaf = 0.0 if children_of(RELAY, child, limit) else 2.0
+                heapq.heappush(waiting, (now + hop_time(child - k) + leaf, len(sent), ch, sign, limit, child, cp))
+
+        for ch in range(CHUNKS):
+            for sign, limit in limits(ch):
+                pass_on(ch, sign, limit, 0, t + 0.3 * ch)
         block_here(0, CHUNKS)
-        lax.fori_loop(0, nz, spread_block, 0)
-        while flying:
-            t += step_time
-            yield t
-            following, landed = [], []
-            for ch, sign, limit, k, near, far in flying:
-                if far is not None:
-                    far.wait_recv()
-                    following.append(pass_on(ch, sign, limit, k + 2))
-                    landed.append((-sign * (k + 2)) % nz)
-                if near is not None:
-                    near.wait_recv()
-                    landed.append((-sign * (k + 1)) % nz)
-            flying = following
-            for block in landed:
-                block_here(block, 1)
-        yield from until("w", t)
+        while waiting:
+            yield waiting[0][0]
+            now, _, ch, sign, limit, k, cp = heapq.heappop(waiting)
+            cp.wait_recv()
+            pass_on(ch, sign, limit, k, now)
+            block_here((-sign * k) % nz, 1)
+        yield from until("w", now)
         flags.add("h")
 
     def tile_exchange(make_src, make_dst, toward):
@@ -340,22 +345,25 @@
                 yield due
 
     def v_path():
-        yield 0.0
         for stage, reach in enumerate((2, 4)):
             for sign in (1, -1):
                 pl.semaphore_signal(know.at[stage], inc=1, device_id=zdev(sign * reach), device_id_type=MESH_ID)
-            yield (1.6, 4.5)[stage]
+            yield (1.5, 4.0)[stage]
             pl.semaphore_wait(know.at[stage], 2)
         finish = tile_exchange(val_src, val_dst, lambda j: nz - j)
-        yield 12.5
+        yield 13.5
         finish()
-        yield from both(lambda half: plane_gather(v_slices, half, 12.5, 3.4, 5.5, 1.5))
+        yield from both(lambda half: plane_gather(v_slices, half, 13.5, 3.5, 6.0, 2.0))
         flags.add("v")
 
     w_slices = (w_piece, w_row, w_col)
 
+    def spread_path():
+        yield 0.2
+        lax.fori_loop(0, nz, spread_block, 0)
+
     def w_path():
-        yield from both(lambda half: plane_gather(w_slices, half, 0.0, 3.5, 8.0, 1.7))
+        yield from both(lambda half: plane_gather(w_slices, half, 0.0, 3.5, 9.0, 2.0))
         flags.add("w")
         for block in pending:
             accumulate(block)
@@ -404,52 +412,48 @@
     def i_chunk(block, ch):
         return iterm.at[wrap(z + block, nz), pl.ds(span * ch, span), :]
 
-    def slots(buf, sign, at, ch):
-        return buf.at[(1 - sign) // 2, at, pl.ds(span * ch, span), :]
-
-    def hidden_relay(t, step_time):
+    def hidden_relay(t):
         yield from until("v", t)
         gate_gradient()
         flags.add("g")
-        todo = [(ch, sign, limit) for ch in range(CHUNKS) for sign, limit in limits(ch)]
-        far, near = {}, {}
-
-        def start(ch, sign, dist, step):
-            need_iterm(sign * dist)
-            cps, buf = (far, ri_even) if step == 2 else (near, ri_odd)
-            cps[ch, sign] = send(i_chunk(sign * dist, ch), slots(buf, sign, (dist - 1) // 2, ch), zdev(step * sign))
-
-        for ch, sign, limit in todo:
-            if limit == 8:
-                start(ch, sign, 8, 2)
-            start(ch, sign, 7, 1)
-        for dist in (6, 4, 2, 0):
-            for ch, sign, limit in todo:
-                need_iterm(sign * dist)
-                if dist:
-                    need_iterm(sign * (dist - 1))
-            t += step_time
-            yield t
-            for ch, sign, limit in todo:
-                here = pl.ds(span * ch, span)
-                side = (1 - sign) // 2
-                q = wrap(z + sign * dist, nz)
-                total = iterm[q, here, :].astype(F32)
-                if (ch, sign) in far:
-                    far[ch, sign].wait_recv()
-                    total = total + ri_even[side, (dist + 1) // 2, here, :].astype(F32)
-                near[ch, sign].wait_recv()
-                total = total + ri_odd[side, dist // 2, here, :].astype(F32)
-                if dist:
+        ready = []
+        flying = {}
+
+        def mature(ch, sign, limit, k):
+            kids = children_of(RING, k, limit)
+            return max((mature(ch, sign, limit, kid) + hop_time(kid - k) for kid in kids), default=0.3 * ch)
+
+        def depth(ch, k):
+            return 0 if k == 0 else depth(ch, RING[k]) + 1
+
+        for ch in range(CHUNKS):
+            for sign, limit in limits(ch):
+                for k in range(limit + 1):
+                    ready.append((mature(ch, sign, limit, k), -depth(ch, k), len(ready), ch, sign, limit, k))
+        ends = {}
+        start = t + 0.5
+        for when, _, _, ch, sign, limit, k in sorted(ready):
+            yield start + when
+            need_iterm(sign * k)
+            here = pl.ds(span * ch, span)
+            side = (1 - sign) // 2
+            q = wrap(z + sign * k, nz)
+            kids = children_of(RING, k, limit)
+            if kids:
+                total = iterm[q, here, :].astype(F32) if k or ch not in ends else gin[here, :]
+                for kid in kids:
+                    flying[ch, sign, kid].wait_recv()
+                    total = total + ri[side, kid - 1, here, :].astype(F32)
+                if k:
                     iterm[q, here, :] = total.astype(BF)
-                    start(ch, sign, dist, 2)
-                    start(ch, sign, dist - 1, 1)
-                elif sign == limits(ch)[0][0]:
-                    held = total
-                    gin[here, :] = held
+                elif ch in ends:
+                    gh_out[here, :] = total.astype(BF)
                 else:
-                    total = total - iterm[q, here, :].astype(F32) + gin[here, :]
-                    gh_out[here, :] = total.astype(BF)
+                    gin[here, :] = total
+                    ends[ch] = True
+            if k:
+                parent = RING[k]
+                flying[ch, sign, k] = send(i_chunk(sign * k, ch), ri.at[side, k - 1, here, :], zdev(sign * (k - parent)))
 
     def plane_reduce(slices, half, bufs, t, small, large, finish):
         piece, row, col = slices
@@ -501,7 +505,7 @@
     g_slices = t_slices(gvals)
 
     def t_half(half):
-        yield 20.5
+        yield 22.0
         t_swap[half].wait_recv()
         here = pl.ds(4 * half, 4)
         tsum[here] = (tterm[jset(c, half)].astype(F32) + tr0[here].astype(F32)).astype(BF)
@@ -511,18 +515,17 @@
 
         yield from plane_reduce(
             (ts_piece, ts_row, ts_col), half, (tr_row if half == 0 else tr_col, tr_piece.at[half]),
-            20.5, 3.6, 5.6, finish,
+            22.0, 4.0, 6.0, finish,
         )
 
     def t_path():
-        yield from until("h", 18.0)
+        yield from until("h", 18.5)
         value_terms()
         yield from both(t_half)
         done = tile_exchange(g_src_fixed, g_dst, lambda j: j)
-        yield 37.5
+        yield 40.0
         done()
-        yield from both(lambda half: plane_gather(g_slices, half, 37.5, 3.4, 5.5, 1.5))
-        gvals_out[...] = gvals[...]
+        yield from both(lambda half: plane_gather(g_slices, half, 40.0, 3.5, 5.5, 2.0))
 
     def ps_piece(yy, xx, half):
         return psum.at[yy, xx, pl.ds(128 * half, 128), :]
@@ -535,14 +538,14 @@
 
     def p_half(half):
         here = pl.ds(128 * half, 128)
-        yield from until("g", 24.5 + half)
-        yield 25.0 + half
+        yield from until("g", 25.5 + half)
+        yield 28.2 + half
         for q in range(nz):
             pterm[q // NX, q % NX, here, :] = jnp.dot(ggt[here, :], hid[q], preferred_element_type=F32).astype(BF)
         swap = send(
             pterm.at[:, :, here, pl.ds(mult(128 * oc, 128), 128)], pr0.at[half], partner
         )
-        yield 28.0 + half
+        yield 32.0 + half
         swap.wait_recv()
         own = pterm[:, :, here, pl.ds(mult(128 * c, 128), 128)]
         psum[:, :, here, :] = (own.astype(F32) + pr0[half].astype(F32)).astype(BF)
@@ -551,12 +554,12 @@
             gg_out[:, pl.ds(128 * half, 128)] = total.T
 
         yield from plane_reduce(
-            (ps_piece, ps_row, ps_col), half, (pr_bundle.at[half], pr_piece.at[half]), 28.0 + half, 4.3, 8.3, finish
+            (ps_piece, ps_row, ps_col), half, (pr_bundle.at[half], pr_piece.at[half]), 32.0 + half, 4.5, 8.5, finish
         )
 
     def aff_path():
-        yield from until("g", 25.0)
-        yield 26.5
+        yield from until("g", 26.0)
+        yield 30.0
         lane = jnp.bitwise_and(idx[...], 127)
         chunk = lax.shift_right_logical(idx[...], 7)
         acc = jnp.zeros((rows_blk, 128), F32)
@@ -568,14 +571,14 @@
         for i in range(nz):
             affp[i] = acc_t[2 * i : 2 * i + 2, :]
         cps = [send(affp.at[wrap(z + k, nz)], affr.at[k], zdev(k)) for k in range(1, nz)]
-        yield 35.0
+        yield 38.5
         total = affp[z]
         for k in range(1, nz):
             cps[k - 1].wait_recv()
             total = total + affr[k]
         affall[z] = total
         cps = [send(affall.at[z], affall.at[z], zdev(k)) for k in range(1, nz)]
-        yield 43.0
+        yield 46.5
         for cp in cps:
             cp.wait_recv()
         for i in range(nz):
@@ -585,7 +588,7 @@
         gs_out[...] = weights * (aff - jnp.sum(weights * aff, axis=0, keepdims=True))
 
     run_streams(
-        [hid_relay(0.0, 4.0), w_path(), v_path(), t_path(), hidden_relay(23.0, 4.0), p_half(0), p_half(1), aff_path()]
+        [v_path(), hid_relay(0.0), w_path(), spread_path(), t_path(), hidden_relay(25.2), p_half(0), p_half(1), aff_path()]
     )
 
     for cp in sent:
@@ -640,10 +643,8 @@
         vm((3, 4, 2, 16, cols), BF),
         vm((2, 3, 4, 16, 128), BF),
         vm((8, 16, 128), BF),
-        vm((nz, 2, NX, 16, cols), BF),
         vm((nz, rows, cols), BF),
-        vm((2, nz // 4, rows, cols), BF),
-        vm((2, nz // 4, rows, cols), BF),
+        vm((2, nz // 2, rows, cols), BF),
         vm((nz, 2, 128), F32),
         vm((nz, 2, 128), F32),
         vm((nz, 2, 128), F32),
@@ -667,7 +668,7 @@
             jax.ShapeDtypeStruct((32, rows), F32),
         ),
         in_specs=[pl.BlockSpec(memory_space=pltpu.HBM)] * 6,
-        out_specs=(vmem,) * 5,
+        out_specs=(vmem, vmem, vmem, hbm, vmem),
         scratch_shapes=scratch,
         compiler_params=pltpu.CompilerParams(
             collective_id=0, has_side_effects=True, vmem_limit_bytes=32 * 1024 * 1024

time: 80 us -> 76.9 us (0.961); the launches traced: 79.8 us -> 75.6 us
  Pallas kernels: 79.2 us -> 75 us
    pallas_call x1, Pallas kernels: 77.6 us -> 73.4 us  [layer(): pl.pallas_call(functools.partial(body, nz), out_shape=(jax.ShapeDtypeStru...]
where the time goes in v3:
time: 76.9 us; the launch traced here: 75.6 us
  Pallas kernels  75 us (98%)
    pallas_call x1, Pallas kernels, layer(): pl.pallas_call(functools.partial(body, nz), out_shape=(jax.ShapeDtypeStru...  73.4 us
    pallas_call x1, Pallas kernels, layer(): pl.pallas_call(functools.partial(write_out, nz), out_shape=(jax.ShapeDtyp...  1.57 us

profile of v3, /device:TPU:1, one launch (start us, length us, event | category | flops | bytes accessed | tf_op | source)
XLA Modules:
  0.0 75.6 jit_solution(16964775033653322922)
XLA Ops:
  0.6 73.4 %shard_map.101 = (bf16[128,256]{1,0:T(8,128)(2,1)S(1)}, bf16[128,256]{1,0:T(8,128)(2,1)S(1)}, f32[128,256]{1,0:T(8,128)S(1)}, bf16[16,2,4,16,256]{4,3,2,1,0:T(8,128)(2,1)S(1)}, f32[32,128]{1,0:T(8,128)S(1)}) custom-call(bf16[128,256]{1,0:T(8,128)(2,1)} %hid_in.1, bf16[128,256]{1,0:T(8,128)(2,1)} %w_in.1, bf16[128,4096]{1,0:T(8,128)(2,1)} %val_in.1, ...), custom_call_target="tpu_custom_call" | custom-call | tf_op jit(solution)/shard_map/pallas_call | solution.py:661
  74.0 1.6 %shard_map.102 = (bf16[128,256]{1,0:T(8,128)(2,1)}, bf16[128,256]{1,0:T(8,128)(2,1)}, f32[128,256]{1,0:T(8,128)}, f32[128,4096]{1,0:T(8,128)}, f32[32,128]{1,0:T(8,128)}) custom-call(bf16[128,256]{1,0:T(8,128)(2,1)S(1)} %get-tuple-element.15.bo_in, bf16[128,256]{1,0:T(8,128)(2,1)S(1)} %get-tuple-element.16.gh_in, f32[128,256]{1,0:T(8,128)S(1)} %get-tuple-element.17.gg_in, ...), custom_call_target="tpu_custom_call" | custom-call | tf_op jit(solution)/shard_map/pallas_call | solution.py:677

commit v4 on v3

--- a/solution.py
+++ b/solution.py
@@ -16,6 +16,7 @@
 CHUNKS = 4
 N_COPIES = 320
 N_LOCAL = 16
+T0 = 22.0
 NT = (((1,), (1,)), ((), ()))
 RELAY = {1: 0, 2: 0, 3: 2, 4: 2, 5: 4, 6: 4, 7: 6, 8: 6}
 RING = {k: k - 1 for k in range(1, 9)}
@@ -56,7 +57,7 @@
     bo_out, gh_out, gg_out, gvals, gs_out,
     hid, wts, vals, spread, spread_t, go, gin, mg, gg, ggt, pad_a, picks, rel_t, wgt, idx,
     pterm, pr0, psum, pr_bundle, pr_piece,
-    tterm, tr0, tsum, tr_row, tr_col, tr_piece, tfin,
+    pair_t, pair_mg, tsum, tr_row, tr_col, tr_piece, tfin,
     iterm, ri, affp, affr, affall, afft,
     send_sem, recv_sem, local_sem, know,
 ):
@@ -112,32 +113,20 @@
         sent.append(cp)
         return cp
 
+    own_h = lcopy(hid_in, hid.at[z])
+    own_w = lcopy(w_in, wts.at[y, x, c])
     own_rows = lcopy(rows_in, picks)
     own_scores = lcopy(score_in, wgt)
-    own_w = lcopy(w_in, wts.at[y, x, c])
-    own_h = lcopy(hid_in, hid.at[z])
     own_g = lcopy(go_in, go)
 
     ylow = lax.rem(y, 2)
     yhigh = lax.div(y, 2)
 
-    pad_a[...] = jnp.zeros_like(pad_a)
-    own_rows.wait()
-    own_scores.wait()
-    pad_a[0:32, :] = picks[...].astype(F32)
     total_rows = nz * rows_blk
 
     def relative(row_f):
         shifted = row_f.astype(jnp.int32) + (total_rows - rows_blk * z)
         return jnp.where(shifted >= total_rows, shifted - total_rows, shifted)
-
-    idx[...] = relative(pad_a[...].T)
-    rel_t[...] = relative(pad_a[0:32, :])
-    scores = wgt[...]
-    expo = jnp.exp(scores - jnp.max(scores, axis=0, keepdims=True))
-    wgt[...] = expo / jnp.sum(expo, axis=0, keepdims=True)
-    weights_bf = wgt[...].astype(BF).astype(F32)
-    afft[...] = weights_bf
 
     def spread_block(i, carry):
         ids = lax.broadcasted_iota(jnp.int32, (rows_blk, rows_blk), 0) + i * rows_blk
@@ -148,9 +137,7 @@
         spread[:, pl.ds(mult(i * rows_blk, rows_blk), rows_blk)] = acc.T.astype(BF)
         return carry
 
-    own_w.wait()
     own_h.wait()
-    own_g.wait()
     pl.semaphore_wait(barrier, len(peers))
 
     def w_piece(yy, xx, cc, half):
@@ -360,9 +347,25 @@
 
     def spread_path():
         yield 0.2
+        pad_a[...] = jnp.zeros_like(pad_a)
+        own_rows.wait()
+        own_scores.wait()
+        pad_a[0:32, :] = picks[...].astype(F32)
+        idx[...] = relative(pad_a[...].T)
+        rel_t[...] = relative(pad_a[0:32, :])
+        scores = wgt[...]
+        expo = jnp.exp(scores - jnp.max(scores, axis=0, keepdims=True))
+        wgt[...] = expo / jnp.sum(expo, axis=0, keepdims=True)
+        afft[...] = wgt[...].astype(BF).astype(F32)
         lax.fori_loop(0, nz, spread_block, 0)
+        own_g.wait()
+        pair_t[:, :, 0:128] = spread_t[pl.ds(8 * (1 - c), 8)]
+        share = send(spread_t.at[pl.ds(8 * (1 - oc), 8)], pair_t.at[:, :, pl.ds(128, 128)], partner)
+        yield 8.0
+        share.wait_recv()
 
     def w_path():
+        own_w.wait()
         yield from both(lambda half: plane_gather(w_slices, half, 0.0, 3.5, 9.0, 2.0))
         flags.add("w")
         for block in pending:
@@ -379,14 +382,8 @@
     def value_terms():
         gate, sig, upstream = gate_parts()
         mg[...] = (upstream * (gate * sig)).astype(BF)
-        for owner in (oc, c):
-            for jl in range(8):
-                j = 8 * (1 - owner) + jl
-                tterm[j] = (
-                    jnp.dot(spread_t[j], mg[...], preferred_element_type=F32).astype(BF).reshape(2, NX, 16, cols)
-                )
-            if not t_swap:
-                t_swap.extend(send(tterm.at[jset(oc, h)], tr0.at[pl.ds(4 * h, 4)], partner) for h in (0, 1))
+        pair_mg[0:128, :] = mg[...]
+        t_swap.append(send(mg, pair_mg.at[pl.ds(128, 128)], partner))
 
     def gate_gradient():
         gate, sig, upstream = gate_parts()
@@ -505,17 +502,20 @@
     g_slices = t_slices(gvals)
 
     def t_half(half):
-        yield 22.0
-        t_swap[half].wait_recv()
+        yield T0
+        if half == 0:
+            t_swap[0].wait_recv()
         here = pl.ds(4 * half, 4)
-        tsum[here] = (tterm[jset(c, half)].astype(F32) + tr0[here].astype(F32)).astype(BF)
+        for jl in range(4 * half, 4 * half + 4):
+            part = jnp.dot(pair_t[jl], pair_mg[...], preferred_element_type=F32)
+            tsum[jl] = part.astype(BF).reshape(2, NX, 16, cols)
 
         def finish(total):
             tfin[here] = total.astype(BF)
 
         yield from plane_reduce(
             (ts_piece, ts_row, ts_col), half, (tr_row if half == 0 else tr_col, tr_piece.at[half]),
-            22.0, 4.0, 6.0, finish,
+            T0, 4.0, 6.0, finish,
         )
 
     def t_path():
@@ -523,9 +523,9 @@
         value_terms()
         yield from both(t_half)
         done = tile_exchange(g_src_fixed, g_dst, lambda j: j)
-        yield 40.0
+        yield T0 + 18.0
         done()
-        yield from both(lambda half: plane_gather(g_slices, half, 40.0, 3.5, 5.5, 2.0))
+        yield from both(lambda half: plane_gather(g_slices, half, T0 + 18.0, 3.5, 5.5, 2.0))
 
     def ps_piece(yy, xx, half):
         return psum.at[yy, xx, pl.ds(128 * half, 128), :]
@@ -636,8 +636,8 @@
         vm((NY, NX, cols, 128), BF),
         vm((2, 3, 4, 128, 128), BF),
         vm((2, 3, 128, 128), BF),
-        vm((nz, 2, NX, 16, cols), BF),
-        vm((8, 2, NX, 16, cols), BF),
+        vm((8, rows, 2 * rows), BF),
+        vm((2 * rows, cols), BF),
         vm((8, 2, NX, 16, cols), BF),
         vm((3, 4, NX, 16, 128), BF),
         vm((3, 4, 2, 16, cols), BF),

time: 76.9 us -> 76.3 us (level)
  no operation moved by 1% of the time
where the time goes in v4:
time: 76.3 us; the launch traced here: 75.2 us
  Pallas kernels  74.5 us (98%)
    pallas_call x1, Pallas kernels, layer(): pl.pallas_call(functools.partial(body, nz), out_shape=(jax.ShapeDtypeStru...  72.9 us
    pallas_call x1, Pallas kernels, layer(): pl.pallas_call(functools.partial(write_out, nz), out_shape=(jax.ShapeDtyp...  1.57 us

profile of v4, /device:TPU:1, one launch (start us, length us, event | category | flops | bytes accessed | tf_op | source)
XLA Modules:
  0.0 75.2 jit_solution(366765566224582719)
XLA Ops:
  0.6 72.9 %shard_map.101 = (bf16[128,256]{1,0:T(8,128)(2,1)S(1)}, bf16[128,256]{1,0:T(8,128)(2,1)S(1)}, f32[128,256]{1,0:T(8,128)S(1)}, bf16[16,2,4,16,256]{4,3,2,1,0:T(8,128)(2,1)S(1)}, f32[32,128]{1,0:T(8,128)S(1)}) custom-call(bf16[128,256]{1,0:T(8,128)(2,1)} %hid_in.1, bf16[128,256]{1,0:T(8,128)(2,1)} %w_in.1, bf16[128,4096]{1,0:T(8,128)(2,1)} %val_in.1, ...), custom_call_target="tpu_custom_call" | custom-call | tf_op jit(solution)/shard_map/pallas_call | solution.py:661
  73.6 1.6 %shard_map.102 = (bf16[128,256]{1,0:T(8,128)(2,1)}, bf16[128,256]{1,0:T(8,128)(2,1)}, f32[128,256]{1,0:T(8,128)}, f32[128,4096]{1,0:T(8,128)}, f32[32,128]{1,0:T(8,128)}) custom-call(bf16[128,256]{1,0:T(8,128)(2,1)S(1)} %get-tuple-element.15.bo_in, bf16[128,256]{1,0:T(8,128)(2,1)S(1)} %get-tuple-element.16.gh_in, f32[128,256]{1,0:T(8,128)S(1)} %get-tuple-element.17.gg_in, ...), custom_call_target="tpu_custom_call" | custom-call | tf_op jit(solution)/shard_map/pallas_call | solution.py:677

commit v5 on v4

--- a/solution.py
+++ b/solution.py
@@ -55,7 +55,7 @@
     nz,
     hid_in, w_in, val_in, rows_in, score_in, go_in,
     bo_out, gh_out, gg_out, gvals, gs_out,
-    hid, wts, vals, spread, spread_t, go, gin, mg, gg, ggt, pad_a, picks, rel_t, wgt, idx,
+    hid, wts, vals, spread, spread_t, go, gin, silu, lift, mg, gg, ggt, pad_a, picks, rel_t, wgt, idx,
     pterm, pr0, psum, pr_bundle, pr_piece,
     pair_t, pair_mg, tsum, tr_row, tr_col, tr_piece, tfin,
     iterm, ri, affp, affr, affall, afft,
@@ -384,13 +384,14 @@
         mg[...] = (upstream * (gate * sig)).astype(BF)
         pair_mg[0:128, :] = mg[...]
         t_swap.append(send(mg, pair_mg.at[pl.ds(128, 128)], partner))
+        silu[...] = gate * sig
+        lift[...] = upstream * (sig * (1.0 + gate * (1.0 - sig)))
 
     def gate_gradient():
-        gate, sig, upstream = gate_parts()
         memory_read = jnp.dot(spread[...], vals[...].reshape(total_rows, cols), preferred_element_type=F32)
-        bo_out[...] = (memory_read * (gate * sig)).astype(BF)
-        slope = (upstream * memory_read * (sig * (1.0 + gate * (1.0 - sig)))).astype(BF)
+        slope = (memory_read * lift[...]).astype(BF)
         gg[...] = slope
+        bo_out[...] = (memory_read * silu[...]).astype(BF)
         ggt[...] = slope.astype(F32).T.astype(BF)
 
     def make_iterm(block):
@@ -622,6 +623,8 @@
         vm((rows, nz * rows), BF),
         vm((nz, rows, rows), BF),
         vm((rows, cols), BF),
+        vm((rows, cols), F32),
+        vm((rows, cols), F32),
         vm((rows, cols), F32),
         vm((rows, cols), BF),
         vm((rows, cols), BF),

time: 76.3 us -> 76.3 us (level)
  no operation moved by 1% of the time
where the time goes in v5:
time: 76.3 us; the launch traced here: 75.2 us
  Pallas kernels  74.6 us (98%)
    pallas_call x1, Pallas kernels, layer(): pl.pallas_call(functools.partial(body, nz), out_shape=(jax.ShapeDtypeStru...  73 us
    pallas_call x1, Pallas kernels, layer(): pl.pallas_call(functools.partial(write_out, nz), out_shape=(jax.ShapeDtyp...  1.57 us

profile of v5, /device:TPU:1, one launch (start us, length us, event | category | flops | bytes accessed | tf_op | source)
XLA Modules:
  0.0 75.2 jit_solution(8372650374421708746)
XLA Ops:
  0.6 73.0 %shard_map.101 = (bf16[128,256]{1,0:T(8,128)(2,1)S(1)}, bf16[128,256]{1,0:T(8,128)(2,1)S(1)}, f32[128,256]{1,0:T(8,128)S(1)}, bf16[16,2,4,16,256]{4,3,2,1,0:T(8,128)(2,1)S(1)}, f32[32,128]{1,0:T(8,128)S(1)}) custom-call(bf16[128,256]{1,0:T(8,128)(2,1)} %hid_in.1, bf16[128,256]{1,0:T(8,128)(2,1)} %w_in.1, bf16[128,4096]{1,0:T(8,128)(2,1)} %val_in.1, ...), custom_call_target="tpu_custom_call" | custom-call | tf_op jit(solution)/shard_map/pallas_call | solution.py:664
  73.6 1.6 %shard_map.102 = (bf16[128,256]{1,0:T(8,128)(2,1)}, bf16[128,256]{1,0:T(8,128)(2,1)}, f32[128,256]{1,0:T(8,128)}, f32[128,4096]{1,0:T(8,128)}, f32[32,128]{1,0:T(8,128)}) custom-call(bf16[128,256]{1,0:T(8,128)(2,1)S(1)} %get-tuple-element.15.bo_in, bf16[128,256]{1,0:T(8,128)(2,1)S(1)} %get-tuple-element.16.gh_in, f32[128,256]{1,0:T(8,128)S(1)} %get-tuple-element.17.gg_in, ...), custom_call_target="tpu_custom_call" | custom-call | tf_op jit(solution)/shard_map/pallas_call | solution.py:680
